TPU v7x, 128 devices: a whole 4x4x4 slice. The times are simulated.
128 devices in a mesh: pitch: 16 (over x, z), span: 8 (over y, core).
Axes of the slice: x: 4, y: 4, z: 4, core: 2. Of those that a mesh axis runs over, the one named last changes fastest.
Arguments:
- stator_state: float32 [5, 16, 512, 2048], P(None, None, 'span', 'pitch'), may hold values from -6 to 6
- rotor_state: float32 [5, 16, 512, 2048], P(None, None, 'span', 'pitch'), may hold values from -6 to 6
- jacobians: float32 [3, 5, 5], replicated, may hold values from -2.5 to 2.5
- field_mix: float32 [5, 5], replicated, may hold values from -2.5 to 2.5
- mode_blend: float32 [5, 2048], replicated, may hold values from 0.1 to 0.9
- rotor_offset: int32 [1], replicated, may hold values from 0 to 2047
Outputs:
- stator_next: float32 [5, 16, 512, 2048], P(None, None, 'span', 'pitch')
- rotor_next: float32 [5, 16, 512, 2048], P(None, None, 'span', 'pitch')
Inputs may be any that keep to these rules, and one draw needn't show every extreme that they name: `rotor_offset`: the rotor's rotation against the stator, in whole pitch cells.
All inputs are finite; a program needn't handle non-finite values.
Results may differ from a plain program's by a relative error of at most 0.0001.
Values sent between devices are 32-bit elements; how exact they have to be, the bound alone decides.
A program may use at most 192 MiB of HBM per device.

v0:
```python
import math

import jax
import jax.numpy as jnp
from jax import lax
from jax.sharding import PartitionSpec as P

NP = 2048


time_step = 0.5
damping = 1.0 / 32.0
highest = lax.Precision.HIGHEST


def padded_2(block, sides, width):
    for axis, dim in sides:
        count = lax.axis_size(axis)
        forward = [(i, i + 1) for i in range(count - 1)]
        forward.append((count - 1, 0))
        backward = [(target, source) for source, target in forward]
        low = lax.ppermute(
            lax.slice_in_dim(block, block.shape[dim] - width, None, axis=dim), axis, forward
        )
        high = lax.ppermute(lax.slice_in_dim(block, 0, width, axis=dim), axis, backward)
        block = jnp.concatenate([low, block, high], axis=dim)
    return block


def hartley_table(row_ids, col_ids, offset):
    products = (row_ids[:, None] + offset) % NP * col_ids[None, :] % NP
    angles = products.astype(jnp.float32) * (2.0 * math.pi / NP)
    return jnp.cos(angles) + jnp.sin(angles)


def contract_last(left, right):
    return lax.dot_general(
        left, right, (((1,), (1,)), ((), ())), precision=highest, preferred_element_type=jnp.float32
    )


def close_span(padded):
    span_pos = lax.axis_index("span")
    last_span = lax.axis_size("span") - 1
    lower_keep = jnp.where(span_pos == 0, 0.0, 1.0)
    upper_keep = jnp.where(span_pos == last_span, 0.0, 1.0)
    extent = padded.shape[2]
    indices = jnp.arange(extent, dtype=jnp.int32)
    rim_scale = jnp.where(
        indices < 2, lower_keep, jnp.where(indices >= extent - 2, upper_keep, 1.0)
    )
    return padded * rim_scale[None, None, :, None]


def update_block(state, extended, jacobians):
    centre = extended[:, 2:-2, 2:-2, 2:-2]
    neighbours = (
        (
            extended[:, 3:-1, 2:-2, 2:-2],
            extended[:, 1:-3, 2:-2, 2:-2],
            extended[:, 4:, 2:-2, 2:-2],
            extended[:, :-4, 2:-2, 2:-2],
        ),
        (
            extended[:, 2:-2, 3:-1, 2:-2],
            extended[:, 2:-2, 1:-3, 2:-2],
            extended[:, 2:-2, 4:, 2:-2],
            extended[:, 2:-2, :-4, 2:-2],
        ),
        (
            extended[:, 2:-2, 2:-2, 3:-1],
            extended[:, 2:-2, 2:-2, 1:-3],
            extended[:, 2:-2, 2:-2, 4:],
            extended[:, 2:-2, 2:-2, :-4],
        ),
    )
    slopes = []
    smoothing = jnp.zeros_like(centre)
    for plus_one, minus_one, plus_two, minus_two in neighbours:
        slopes.append(0.5 * (plus_one - minus_one))
        smoothing = smoothing + (
            plus_two - 4.0 * plus_one + 6.0 * centre - 4.0 * minus_one + minus_two
        )
    changes = []
    for target in range(state.shape[0]):
        totals = -damping * smoothing[target]
        for course in range(3):
            for source in range(state.shape[0]):
                totals = totals - jacobians[course, target, source] * slopes[course][source]
        changes.append(totals)
    return state + time_step * jnp.stack(changes)


def shards(stator_state, rotor_state, jacobians, field_mix, mode_blend, rotor_offset):
    fields, axial_cells, span_rows, pitch_cells = stator_state.shape
    offset = rotor_offset[0]
    position = lax.axis_index("pitch")
    stator_planes = jnp.stack(
        [stator_state[:, axial_cells - 1], stator_state[:, axial_cells - 2]], axis=0
    )
    rotor_planes = jnp.stack([rotor_state[:, 0], rotor_state[:, 1]], axis=0)
    planes = jnp.stack([stator_planes, rotor_planes], axis=0)
    plane_rows = 2 * fields * span_rows
    stacked = planes.reshape(2, plane_rows, pitch_cells)
    mode_index = jnp.arange(NP, dtype=jnp.int32)
    my_range = position * pitch_cells + jnp.arange(pitch_cells, dtype=jnp.int32)
    piece_rows = lax.all_gather(stacked, "pitch", axis=2, tiled=True)
    amount = piece_rows.shape[2]
    angles = jnp.arange(amount, dtype=jnp.int32)
    stator_matrix = hartley_table(angles, mode_index, 0)
    rotor_matrix = hartley_table(angles, mode_index, offset)
    stator_modes = jnp.dot(
        piece_rows[0], stator_matrix, precision=highest, preferred_element_type=jnp.float32
    )
    rotor_modes = jnp.dot(
        piece_rows[1], rotor_matrix, precision=highest, preferred_element_type=jnp.float32
    )
    blend = mode_blend[None, :, None, :]
    stator_modes = stator_modes.reshape(2, fields, span_rows, NP)
    rotor_modes = rotor_modes.reshape(2, fields, span_rows, NP)
    stator_blend = (blend * rotor_modes + (1.0 - blend) * stator_modes).reshape(plane_rows, NP)
    rotor_blend = (blend * stator_modes + (1.0 - blend) * rotor_modes).reshape(plane_rows, NP)
    stator_back = contract_last(stator_blend, hartley_table(my_range, mode_index, 0)) / NP
    rotor_back = contract_last(rotor_blend, hartley_table(my_range, mode_index, offset)) / NP
    inverse = jnp.stack([stator_back, rotor_back]).reshape(2, 2, fields, span_rows, pitch_cells)
    ghosts = jnp.einsum("fg,slgrp->slfrp", field_mix, inverse, precision=highest)
    stator_ghost = jnp.moveaxis(ghosts[0], 0, 1)
    rotor_ghost = jnp.moveaxis(ghosts[1], 0, 1)[:, ::-1]
    ghost_pads = ((0, 0), (0, 0), (2, 2), (2, 2))
    no_inflow = jnp.zeros((fields, 2, span_rows + 4, pitch_cells + 4), jnp.float32)
    stator_padded = close_span(padded_2(stator_state, (("pitch", 3), ("span", 2)), 2))
    rotor_padded = close_span(padded_2(rotor_state, (("pitch", 3), ("span", 2)), 2))
    stator_ext = jnp.concatenate(
        [no_inflow, stator_padded, jnp.pad(stator_ghost, ghost_pads)], axis=1
    )
    rotor_ext = jnp.concatenate([jnp.pad(rotor_ghost, ghost_pads), rotor_padded, no_inflow], axis=1)
    return (
        update_block(stator_state, stator_ext, jacobians),
        update_block(rotor_state, rotor_ext, jacobians),
    )


def solution(mesh):
    in_specs = (P(None, None, "span", "pitch"), P(None, None, "span", "pitch"), P(), P(), P(), P())
    out_specs = (P(None, None, "span", "pitch"), P(None, None, "span", "pitch"))
    return jax.shard_map(shards, mesh=mesh, in_specs=in_specs, out_specs=out_specs, check_vma=False)
```

profile of v0, /device:TPU:1, one launch (start us, length us, event | category | flops | bytes accessed | tf_op | source)
XLA Modules:
  0.0 484.4 jit_solution(2772236273300777699)
XLA Ops:
  7.2 1.2 slice_bitcast_fusion.3
  10.4 3.3 fusion.280
  13.7 2.7 copy.42
  16.5 6.8 %collective-permute-start.5 = (f32[5,16,64,2]{2,1,3,0:T(8,128)S(1)}, f32[5,16,64,2]{2,1,3,0:T(8,128)S(1)}, u32[]{:S(2)}, u32[]{:S(2)}) collective-permute-start(f32[5,16,64,2]{2,1,3,0:T(8,128)S(1)} %copy.42), channel_id=1, source_target_pairs={{8,0},{16,8},{24,16},{32,24},{40,32},{48,40},{56,48},{64,56},{72,6... | collective-permute-start | bytes 122888 | tf_op jit(solution)/shard_map/ppermute | solution.py:25
  23.3 2.8 copy.41
  26.2 3.3 fusion.281
  29.5 2.6 copy.38
  32.1 4.8 collective-permute-start.1
  36.9 3.3 copy.37
  44.0 69.5 %fusion.294 = f32[2048,2048,1,1]{1,0,3,2:T(8,128)} fusion(s32[2048]{0:T(1024)S(1)} %add_select_fusion.5), kind=kLoop, calls=%fused_computation.15.clone.1 | loop fusion | flops 62914560 | bytes 16785408 | tf_op jit(solution)/shard_map/dot_general | solution.py:115
  113.6 69.6 %fusion.7.clone.4 = f32[2048,2048,1,1]{1,0,3,2:T(8,128)} fusion(s32[2048]{0:T(1024)S(1)} %add_select_fusion.4), kind=kLoop, calls=%fused_computation.13.clone.clone.clone.1 | loop fusion | flops 62914560 | bytes 16785408 | tf_op jit(solution)/shard_map/add | solution.py:121
  183.1 3.0 copy.31
  186.1 3.0 copy.24
  189.1 2.5 copy.29
  191.6 2.6 copy.27
  194.1 1.2 pad_maximum_fusion.5
  195.3 1.4 collective-permute-start.7
  196.8 1.2 collective-permute-start.6
  198.0 3.4 copy.18
  201.4 3.3 copy.16
  204.7 1.4 pad_maximum_fusion.8
  206.7 1.3 collective-permute-start.2
  207.9 3.0 collective-permute-done.3
  210.9 10.1 %maximum_multiply_fusion.1 = (f32[5,16,68,132]{3,1,2,0:T(8,128)}, f32[5,16,68,132]{3,1,2,0:T(8,128)}) fusion(f32[5,16,2,132]{3,1,2,0:T(8,128)S(1)} %collective-permute-done.7, f32[5,16,64,2]{3,1,2,0:T(8,128)S(1)} %copy-done.12, f32[5,16,64,128]{3,1,2,0:T(8,128)S(1)} %copy-done.10, f32[5,16,64,2]{3,1,2,0:T(8,128)S(1)} %copy-done.13, ...), kind=kLoop, calls=%fused_computation.47 | loop fusion | flops 7180800 | bytes 11489552 | tf_op jit(solution)/shard_map/mul | solution.py:52
  221.0 7.6 %fusion.279 = (f32[1,640,2048]{2,1,0:T(8,128)S(1)}, f32[1,640,2048]{2,1,0:T(8,128)}) fusion(f32[2,640,2048]{2,1,0:T(8,128)} %all-gather.2.cloned.1.call-done), kind=kLoop, calls=%fused_computation.355 | loop fusion | bytes 20971520 | tf_op jit(solution)/shard_map/slice | solution.py:113
  228.7 39.3 %fusion.8 = f32[2,5,64,2048]{3,2,1,0:T(8,128)} fusion(f32[2,5,64,2048]{3,2,1,0:T(8,128)} %bitcast.148, f32[2048,2048,1,1]{1,0,3,2:T(8,128)} %fusion.294), kind=kOutput, calls=%fused_computation.14 | convolution fusion | flops 32212254720 | bytes 27262976 | tf_op jit(solution)/shard_map/dot_general | solution.py:115
  268.0 37.6 %multiply_add_fusion.1 = (f32[2,5,64,2048]{3,2,1,0:T(8,128)}, f32[2,5,64,2048]{3,2,1,0:T(8,128)}) fusion(f32[2,5,64,2048]{3,2,1,0:T(8,128)} %fusion.8, f32[5,2048]{1,0:T(8,128)S(1)} %broadcast_subtract_fusion, f32[5,2048]{1,0:T(8,128)S(1)} %copy-done.17, f32[2,5,64,2048]{3,2,1,0:T(8,128)S(1)} %bitcast.145, f32[2048,2048,1,1]{1,0,3,2:T(8,128)S(1)} %bitcast.144), kind=kOutput, calls=%fused_computation.49 | convolution fusion | flops 32220119040 | bytes 37830656 | tf_op jit(solution)/shard_map/dot_general | solution.py:112
  305.6 10.9 %convolution_multiply_fusion = f32[640,128]{1,0:T(8,128)S(1)} fusion(f32[640,2048]{1,0:T(8,128)} %bitcast.147, s32[128]{0:T(128)S(1)} %get-tuple-element.107), kind=kOutput, calls=%fused_computation.95 | convolution fusion | flops 2017280000 | bytes 5571072 | tf_op jit(solution)/shard_map/dot_general | solution.py:37
  316.7 8.7 %convolution_multiply_fusion.1 = f32[640,128]{1,0:T(8,128)S(1)} fusion(f32[640,2048]{1,0:T(8,128)S(1)} %bitcast.146, s32[128]{0:T(128)S(1)} %get-tuple-element.108), kind=kOutput, calls=%fused_computation.96 | convolution fusion | flops 2017280000 | bytes 5571072 | tf_op jit(solution)/shard_map/dot_general | solution.py:37
  325.6 1.0 convolution_bitcast_fusion
  327.1 4.6 select_maximum_fusion.1
  331.7 13.5 %subtract_multiply_fusion.5 = (f32[5,16,64,128]{3,1,2,0:T(8,128)S(1)}, f32[5,16,64,128]{3,1,2,0:T(8,128)}, f32[5,16,64,128]{3,1,2,0:T(8,128)}, f32[5,16,64,128]{3,1,2,0:T(8,128)}) fusion(f32[5,18,68,132]{3,1,2,0:T(8,128)} %select_maximum_fusion.1, f32[5,16,68,132]{3,1,2,0:T(8,128)S(1)} %bitcast.142), kind=kLoop, calls=%fused_computation.87 | loop fusion | flops 17694720 | bytes 44892160 | tf_op jit(solution)/shard_map/mul | solution.py:80
  345.3 13.4 %fusion.241 = f32[5,16,64,128]{3,1,2,0:T(8,128)S(1)} fusion(f32[5,16,64,128]{3,1,2,0:T(8,128)} %get-tuple-element.7, f32[5,16,64,128]{3,1,2,0:T(8,128)} %get-tuple-element.19, f32[5,16,64,128]{3,1,2,0:T(8,128)} %get-tuple-element.18, f32[5,16,64,128]{3,1,2,0:T(8,128)S(1)} %get-tuple-element.6, f32[]{:T(128)} %bitcast.36, f32[]{:T(128)} %bitcast.35, ...), kind=kLoop, calls=%fused_computation.289 | loop fusion | flops 4063231 | bytes 8912956
  358.7 9.8 %fusion.225 = f32[5,16,64,128]{3,1,2,0:T(8,128)S(1)} fusion(f32[5,16,64,128]{3,1,2,0:T(8,128)S(1)} %fusion.241, f32[5,16,64,128]{3,1,2,0:T(8,128)S(1)} %copy-done.15, f32[5,16,64,128]{3,1,2,0:T(8,128)S(1)} %copy-done.4, f32[5,16,64,128]{3,1,2,0:T(8,128)S(1)} %copy-done.3, f32[5,16,64,128]{3,1,2,0:T(8,128)S(1)} %get-tuple-element.6, f32[]{:T(128)} %bitcast.51, ...), kind=kLoop, calls=%fused_computation.272 | loop fusion | flops 4063232 | bytes 8912956
  368.4 9.8 %fusion.209 = f32[5,16,64,128]{3,1,2,0:T(8,128)S(1)} fusion(f32[5,16,64,128]{3,1,2,0:T(8,128)S(1)} %fusion.225, f32[5,16,64,128]{3,1,2,0:T(8,128)S(1)} %copy-done.15, f32[5,16,64,128]{3,1,2,0:T(8,128)S(1)} %copy-done.4, f32[5,16,64,128]{3,1,2,0:T(8,128)S(1)} %copy-done.3, f32[5,16,64,128]{3,1,2,0:T(8,128)S(1)} %get-tuple-element.6, f32[]{:T(128)} %bitcast.66, ...), kind=kLoop, calls=%fused_computation.255 | loop fusion | flops 4063232 | bytes 8912956
  378.3 9.9 %fusion.193 = f32[5,16,64,128]{3,1,2,0:T(8,128)S(1)} fusion(f32[5,16,64,128]{3,1,2,0:T(8,128)S(1)} %fusion.209, f32[5,16,64,128]{3,1,2,0:T(8,128)S(1)} %copy-done.15, f32[5,16,64,128]{3,1,2,0:T(8,128)S(1)} %copy-done.4, f32[5,16,64,128]{3,1,2,0:T(8,128)S(1)} %copy-done.3, f32[5,16,64,128]{3,1,2,0:T(8,128)S(1)} %get-tuple-element.6, f32[]{:T(128)} %bitcast.81, ...), kind=kLoop, calls=%fused_computation.238 | loop fusion | flops 4063232 | bytes 8912956
  388.2 10.2 %fusion.177 = f32[5,16,64,128]{3,1,2,0:T(8,128)S(1)} fusion(f32[5,16,64,128]{3,1,2,0:T(8,128)S(1)} %fusion.193, f32[5,16,64,128]{3,1,2,0:T(8,128)S(1)} %copy-done.15, f32[5,16,64,128]{3,1,2,0:T(8,128)S(1)} %copy-done.4, f32[5,16,64,128]{3,1,2,0:T(8,128)S(1)} %copy-done.3, f32[5,16,64,128]{3,1,2,0:T(8,128)S(1)} %get-tuple-element.6, f32[]{:T(128)} %bitcast.96, ...), kind=kLoop, calls=%fused_computation.221 | loop fusion | flops 4063232 | bytes 8912956 | tf_op jit(solution)/shard_map/stack | solution.py:91
  398.4 1.7 multiply_add_fusion.3
  400.1 2.3 copy.32
  402.7 5.9 %select_maximum_fusion = f32[5,18,68,132]{3,1,2,0:T(8,128)} fusion(f32[5,2,64,128]{3,1,2,0:T(2,128)S(1)} %copy.44, f32[5,16,68,132]{3,1,2,0:T(8,128)} %get-tuple-element.105), kind=kLoop, calls=%fused_computation.42 | loop fusion | flops 2423520 | bytes 6431360 | tf_op jit(solution)/shard_map/concatenate | solution.py:136
  408.6 12.6 %subtract_multiply_fusion.2 = (f32[5,16,64,128]{3,1,2,0:T(8,128)S(1)}, f32[5,16,64,128]{3,1,2,0:T(8,128)}, f32[5,16,64,128]{3,1,2,0:T(8,128)S(1)}, f32[5,16,64,128]{3,1,2,0:T(8,128)}) fusion(f32[5,18,68,132]{3,1,2,0:T(8,128)} %select_maximum_fusion, f32[5,16,68,132]{3,1,2,0:T(8,128)S(1)} %bitcast.140), kind=kLoop, calls=%fused_computation.83 | loop fusion | flops 17694720 | bytes 44892160 | tf_op jit(solution)/shard_map/mul | solution.py:80
  421.2 12.3 %fusion.161 = f32[5,16,64,128]{3,1,2,0:T(8,128)S(1)} fusion(f32[5,16,64,128]{3,1,2,0:T(8,128)} %get-tuple-element.5, f32[5,16,64,128]{3,1,2,0:T(8,128)} %get-tuple-element.17, f32[5,16,64,128]{3,1,2,0:T(8,128)S(1)} %get-tuple-element.16, f32[5,16,64,128]{3,1,2,0:T(8,128)S(1)} %get-tuple-element.4, f32[]{:T(128)} %bitcast.36, f32[]{:T(128)} %bitcast.35, ...), kind=kLoop, calls=%fused_computation.203 | loop fusion | flops 4063231 | bytes 8912956
  433.6 9.8 %fusion.145 = f32[5,16,64,128]{3,1,2,0:T(8,128)S(1)} fusion(f32[5,16,64,128]{3,1,2,0:T(8,128)S(1)} %fusion.161, f32[5,16,64,128]{3,1,2,0:T(8,128)S(1)} %copy-done.14, f32[5,16,64,128]{3,1,2,0:T(8,128)S(1)} %copy-done.2, f32[5,16,64,128]{3,1,2,0:T(8,128)S(1)} %get-tuple-element.16, f32[5,16,64,128]{3,1,2,0:T(8,128)S(1)} %get-tuple-element.4, f32[]{:T(128)} %bitcast.51, ...), kind=kLoop, calls=%fused_computation.186 | loop fusion | flops 4063232 | bytes 8912956
  443.4 9.8 %fusion.129 = f32[5,16,64,128]{3,1,2,0:T(8,128)S(1)} fusion(f32[5,16,64,128]{3,1,2,0:T(8,128)S(1)} %fusion.145, f32[5,16,64,128]{3,1,2,0:T(8,128)S(1)} %copy-done.14, f32[5,16,64,128]{3,1,2,0:T(8,128)S(1)} %copy-done.2, f32[5,16,64,128]{3,1,2,0:T(8,128)S(1)} %get-tuple-element.16, f32[5,16,64,128]{3,1,2,0:T(8,128)S(1)} %get-tuple-element.4, f32[]{:T(128)} %bitcast.66, ...), kind=kLoop, calls=%fused_computation.169 | loop fusion | flops 4063232 | bytes 8912956
  453.2 9.9 %fusion.113 = f32[5,16,64,128]{3,1,2,0:T(8,128)S(1)} fusion(f32[5,16,64,128]{3,1,2,0:T(8,128)S(1)} %fusion.129, f32[5,16,64,128]{3,1,2,0:T(8,128)S(1)} %copy-done.14, f32[5,16,64,128]{3,1,2,0:T(8,128)S(1)} %copy-done.2, f32[5,16,64,128]{3,1,2,0:T(8,128)S(1)} %get-tuple-element.16, f32[5,16,64,128]{3,1,2,0:T(8,128)S(1)} %get-tuple-element.4, f32[]{:T(128)} %bitcast.81, ...), kind=kLoop, calls=%fused_computation.152 | loop fusion | flops 4063232 | bytes 8912956
  463.1 10.2 %fusion.97 = f32[5,16,64,128]{3,1,2,0:T(8,128)S(1)} fusion(f32[5,16,64,128]{3,1,2,0:T(8,128)S(1)} %fusion.113, f32[5,16,64,128]{3,1,2,0:T(8,128)S(1)} %copy-done.14, f32[5,16,64,128]{3,1,2,0:T(8,128)S(1)} %copy-done.2, f32[5,16,64,128]{3,1,2,0:T(8,128)S(1)} %get-tuple-element.16, f32[5,16,64,128]{3,1,2,0:T(8,128)S(1)} %get-tuple-element.4, f32[]{:T(128)} %bitcast.96, ...), kind=kLoop, calls=%fused_computation.135 | loop fusion | flops 4063232 | bytes 8912956 | tf_op jit(solution)/shard_map/stack | solution.py:91
  473.3 1.7 multiply_add_fusion.2
  475.0 2.3 copy.33
  (89 shorter events, 6.9 us)
Async XLA Ops:
  7.2 318.5 %copy-start = (f32[5,5]{1,0:T(8,128)S(1)}, f32[5,5]{1,0:T(8,128)}, u32[]{:S(2)}) copy-start(f32[5,5]{1,0:T(8,128)} %param.9) | copy-start | bytes 304
  7.2 3.3 copy-start.7
  7.2 213.8 %all-gather.2.cloned.1.call-start = ((), (), s32[]{:S(2)}) async-start(), calls=%async_computation | async-start | bytes 11141120 | tf_op jit(solution)/shard_map/all_gather | solution.py:107
  13.7 12.4 %copy-start.5 = (f32[5,16,64,128]{3,2,1,0:T(8,128)S(1)}, f32[5,16,64,128]{3,2,1,0:T(8,128)}, u32[]{:S(2)}) copy-start(f32[5,16,64,128]{3,2,1,0:T(8,128)} %param.6) | copy-start | bytes 7864324
  16.5 172.6 %collective-permute-start.5 = (f32[5,16,64,2]{2,1,3,0:T(8,128)S(1)}, f32[5,16,64,2]{2,1,3,0:T(8,128)S(1)}, u32[]{:S(2)}, u32[]{:S(2)}) collective-permute-start(f32[5,16,64,2]{2,1,3,0:T(8,128)S(1)} %copy.42), channel_id=1, source_target_pairs={{8,0},{16,8},{24,16},{32,24},{40,32},{48,40},{56,48},{64,56},{72,6... | collective-permute-start | bytes 122888 | tf_op jit(solution)/shard_map/ppermute | solution.py:25
  26.1 165.5 %collective-permute-start.4 = (f32[5,16,64,2]{2,1,3,0:T(8,128)S(1)}, f32[5,16,64,2]{2,1,3,0:T(8,128)S(1)}, u32[]{:S(2)}, u32[]{:S(2)}) collective-permute-start(f32[5,16,64,2]{2,1,3,0:T(8,128)S(1)} %copy.41), channel_id=1, source_target_pairs={{0,8},{8,16},{16,24},{24,32},{32,40},{40,48},{48,56},{56,64},{64,7... | collective-permute-start | bytes 122888 | tf_op jit(solution)/shard_map/ppermute | solution.py:22
  29.5 11.7 %copy-start.18 = (f32[3,5,5]{2,0,1:T(4,128)S(1)}, f32[3,5,5]{2,0,1:T(4,128)}, u32[]{:S(2)}) copy-start(f32[3,5,5]{2,0,1:T(4,128)} %param.8) | copy-start | bytes 904
  29.5 14.5 %copy-start.17 = (f32[5,2048]{1,0:T(8,128)S(1)}, f32[5,2048]{1,0:T(8,128)}, u32[]{:S(2)}) copy-start(f32[5,2048]{1,0:T(8,128)} %param.10) | copy-start | bytes 122884
  32.1 165.9 %collective-permute-start.1 = (f32[5,16,64,2]{2,1,3,0:T(8,128)S(1)}, f32[5,16,64,2]{2,1,3,0:T(8,128)}, u32[]{:S(2)}, u32[]{:S(2)}) collective-permute-start(f32[5,16,64,2]{2,1,3,0:T(8,128)S(1)} %copy.38), channel_id=1, source_target_pairs={{8,0},{16,8},{24,16},{32,24},{40,32},{48,40},{56,48},{64,56},{72,6... | collective-permute-start | bytes 122888 | tf_op jit(solution)/shard_map/ppermute | solution.py:25
  40.2 161.2 %collective-permute-start = (f32[5,16,64,2]{2,1,3,0:T(8,128)}, f32[5,16,64,2]{2,1,3,0:T(8,128)}, u32[]{:S(2)}, u32[]{:S(2)}) collective-permute-start(f32[5,16,64,2]{2,1,3,0:T(8,128)} %copy.37), channel_id=1, source_target_pairs={{0,8},{8,16},{16,24},{24,32},{32,40},{40,48},{48,56},{56,64},{64,7... | collective-permute-start | bytes 122888 | tf_op jit(solution)/shard_map/ppermute | solution.py:22
  113.6 69.6 %copy-start.8 = (f32[5,16,64,128]{3,2,1,0:T(8,128)S(1)}, f32[5,16,64,128]{3,2,1,0:T(8,128)}, u32[]{:S(2)}) copy-start(f32[5,16,64,128]{3,2,1,0:T(8,128)} %param.7) | copy-start | bytes 7864324
  189.1 5.0 %copy-start.10 = (f32[5,16,64,128]{3,1,2,0:T(8,128)S(1)}, f32[5,16,64,128]{3,1,2,0:T(8,128)}, u32[]{:S(2)}) copy-start(f32[5,16,64,128]{3,1,2,0:T(8,128)} %copy.31) | copy-start | bytes 7864324
  195.3 12.6 %collective-permute-start.7 = (f32[5,16,2,132]{3,1,2,0:T(8,128)S(1)}, f32[5,16,2,132]{3,1,2,0:T(8,128)S(1)}, u32[]{:S(2)}, u32[]{:S(2)}) collective-permute-start(f32[5,16,2,132]{3,1,2,0:T(8,128)S(1)} %get-tuple-element.13), channel_id=1, source_target_pairs={{1,0},{2,1},{3,2},{4,3},{5,4},{6,5},{7,6},{0,7},{9,8},{10,9},{11,1... | collective-permute-start | bytes 253448 | tf_op jit(solution)/shard_map/ppermute | solution.py:25
  196.8 11.1 %collective-permute-start.6 = (f32[5,16,2,132]{3,1,2,0:T(8,128)S(1)}, f32[5,16,2,132]{3,1,2,0:T(8,128)S(1)}, u32[]{:S(2)}, u32[]{:S(2)}) collective-permute-start(f32[5,16,2,132]{3,1,2,0:T(8,128)S(1)} %get-tuple-element.12), channel_id=1, source_target_pairs={{0,1},{1,2},{2,3},{3,4},{4,5},{5,6},{6,7},{7,0},{8,9},{9,10},{10,1... | collective-permute-start | bytes 253448 | tf_op jit(solution)/shard_map/ppermute | solution.py:22
  204.7 6.2 %copy-start.11 = (f32[5,16,64,128]{3,1,2,0:T(8,128)S(1)}, f32[5,16,64,128]{3,1,2,0:T(8,128)}, u32[]{:S(2)}) copy-start(f32[5,16,64,128]{3,1,2,0:T(8,128)} %copy.24) | copy-start | bytes 7864324
  204.7 6.2 %copy-start.12 = (f32[5,16,64,2]{3,1,2,0:T(8,128)S(1)}, f32[5,16,64,2]{3,1,2,0:T(8,128)}, u32[]{:S(2)}) copy-start(f32[5,16,64,2]{3,1,2,0:T(8,128)} %copy.29) | copy-start | bytes 122884
  204.7 6.2 %copy-start.13 = (f32[5,16,64,2]{3,1,2,0:T(8,128)S(1)}, f32[5,16,64,2]{3,1,2,0:T(8,128)}, u32[]{:S(2)}) copy-start(f32[5,16,64,2]{3,1,2,0:T(8,128)} %copy.27) | copy-start | bytes 122884
  206.2 4.8 collective-permute-start.3
  206.7 4.3 collective-permute-start.2
  228.6 39.3 %slice-start.4 = ((s8[16777216]{0:T(1024)(128)(4,1)}), s8[4194304]{0:T(1024)(128)(4,1)S(1)}, s32[]{:S(2)}) async-start(s8[16777216]{0:T(1024)(128)(4,1)} %bitcast.143), calls=%async_computation.5 | async-start | bytes 8388608
  228.6 39.3 %slice-start.5 = ((s8[16777216]{0:T(1024)(128)(4,1)}), s8[4194304]{0:T(1024)(128)(4,1)S(1)}, s32[]{:S(2)}) async-start(s8[16777216]{0:T(1024)(128)(4,1)} %bitcast.143), calls=%async_computation.6 | async-start | bytes 8388608
  228.7 39.3 %slice-start.6 = ((s8[16777216]{0:T(1024)(128)(4,1)}), s8[4194304]{0:T(1024)(128)(4,1)S(1)}, s32[]{:S(2)}) async-start(s8[16777216]{0:T(1024)(128)(4,1)} %bitcast.143), calls=%async_computation.7 | async-start | bytes 8388608
  228.7 39.3 %slice-start.7 = ((s8[16777216]{0:T(1024)(128)(4,1)}), s8[4194304]{0:T(1024)(128)(4,1)S(1)}, s32[]{:S(2)}) async-start(s8[16777216]{0:T(1024)(128)(4,1)} %bitcast.143), calls=%async_computation.8 | async-start | bytes 8388608
  305.6 11.1 %copy-start.16 = (f32[2,5,64,2048]{3,2,1,0:T(8,128)S(1)}, f32[2,5,64,2048]{3,2,1,0:T(8,128)}, u32[]{:S(2)}) copy-start(f32[2,5,64,2048]{3,2,1,0:T(8,128)} %get-tuple-element.8) | copy-start | bytes 15728644
  316.7 10.3 %slice-start.2 = ((s8[5570560]{0:T(1024)(128)(4,1)}), s8[4194304]{0:T(1024)(128)(4,1)S(1)}, s32[]{:S(2)}) async-start(s8[5570560]{0:T(1024)(128)(4,1)} %bitcast.141), calls=%async_computation.3 | async-start | bytes 8388608
  316.7 10.3 %slice-start.3 = ((s8[5570560]{0:T(1024)(128)(4,1)}), s8[1376256]{0:T(1024)(128)(4,1)S(1)}, s32[]{:S(2)}) async-start(s8[5570560]{0:T(1024)(128)(4,1)} %bitcast.141), calls=%async_computation.4 | async-start | bytes 2752512
  345.2 13.4 %copy-start.3 = (f32[5,16,64,128]{3,1,2,0:T(8,128)S(1)}, f32[5,16,64,128]{3,1,2,0:T(8,128)}, u32[]{:S(2)}) copy-start(f32[5,16,64,128]{3,1,2,0:T(8,128)} %get-tuple-element.18) | copy-start | bytes 7864324
  345.2 13.4 %copy-start.4 = (f32[5,16,64,128]{3,1,2,0:T(8,128)S(1)}, f32[5,16,64,128]{3,1,2,0:T(8,128)}, u32[]{:S(2)}) copy-start(f32[5,16,64,128]{3,1,2,0:T(8,128)} %get-tuple-element.19) | copy-start | bytes 7864324
  345.2 13.4 %copy-start.15 = (f32[5,16,64,128]{3,1,2,0:T(8,128)S(1)}, f32[5,16,64,128]{3,1,2,0:T(8,128)}, u32[]{:S(2)}) copy-start(f32[5,16,64,128]{3,1,2,0:T(8,128)} %get-tuple-element.7) | copy-start | bytes 7864324
  388.2 10.2 %copy-start.6 = (f32[5,16,64,128]{3,2,1,0:T(8,128)S(1)}, f32[5,16,64,128]{3,2,1,0:T(8,128)}, u32[]{:S(2)}) copy-start(f32[5,16,64,128]{3,2,1,0:T(8,128)} %param.6) | copy-start | bytes 7864324
  400.1 8.5 %slice-start = ((s8[5570560]{0:T(1024)(128)(4,1)}), s8[1376256]{0:T(1024)(128)(4,1)S(1)}, s32[]{:S(2)}) async-start(s8[5570560]{0:T(1024)(128)(4,1)} %bitcast.139), calls=%async_computation.1 | async-start | bytes 2752512
  402.7 5.9 %slice-start.1 = ((s8[5570560]{0:T(1024)(128)(4,1)}), s8[4194304]{0:T(1024)(128)(4,1)S(1)}, s32[]{:S(2)}) async-start(s8[5570560]{0:T(1024)(128)(4,1)} %bitcast.139), calls=%async_computation.2 | async-start | bytes 8388608
  421.2 12.4 %copy-start.2 = (f32[5,16,64,128]{3,1,2,0:T(8,128)S(1)}, f32[5,16,64,128]{3,1,2,0:T(8,128)}, u32[]{:S(2)}) copy-start(f32[5,16,64,128]{3,1,2,0:T(8,128)} %get-tuple-element.17) | copy-start | bytes 7864324
  421.2 12.4 %copy-start.14 = (f32[5,16,64,128]{3,1,2,0:T(8,128)S(1)}, f32[5,16,64,128]{3,1,2,0:T(8,128)}, u32[]{:S(2)}) copy-start(f32[5,16,64,128]{3,1,2,0:T(8,128)} %get-tuple-element.5) | copy-start | bytes 7864324
  463.1 10.2 %copy-start.9 = (f32[5,16,64,128]{3,2,1,0:T(8,128)S(1)}, f32[5,16,64,128]{3,2,1,0:T(8,128)}, u32[]{:S(2)}) copy-start(f32[5,16,64,128]{3,2,1,0:T(8,128)} %param.7) | copy-start | bytes 7864324
  473.3 4.0 copy-start.1
Sparse Core Ops, SparseCore 0:
  10.6 95.5 all-gather.1
where the time goes:
time: 494 us; the launch traced here: 484 us
  other arithmetic  298 us (60%)
  matrix products  97.5 us (20%)
  local copies, waits for them, and re-layouts  54.1 us (11%)
  starting transfers between devices  16.4 us (3%)
  between operations  15.4 us (3%)
    unnamed x11, other arithmetic  84.8 us
    add x1, other arithmetic, shards(): blend * rotor_modes + (1.0 - blend) * stator_modes  69.6 us
    dot_general x1, other arithmetic, shards(): jnp.dot(piece_rows[1], rotor_matrix, precision=highest, preferred_element...  69.5 us
    dot_general x1, matrix products, shards(): jnp.dot(piece_rows[1], rotor_matrix, precision=highest, preferred_element...  39.3 us
    dot_general x1, matrix products, shards(): jnp.dot(piece_rows[0], stator_matrix, precision=highest, preferred_elemen...  37.6 us
    mul x2, other arithmetic, update_block(): slopes.append(0.5 * (plus_one - minus_one))  26.2 us
    unnamed x64, local copies, waits for them, and re-layouts  22.6 us
    another operation x2, other arithmetic, update_block(): return state + time_step * jnp.stack(changes)  20.4 us
  transfers between devices with their start and end apart: 9, of which 1 were waited for; matrix products, arithmetic and copies ran while one was open for 39% of the time, Pallas kernels for 0%

commit v1 on v0

v1 whole, which is shorter than its diff:
```python
import math

import jax
import jax.numpy as jnp
import ml_dtypes
import numpy as np
from jax import lax
from jax.experimental import pallas as pl
from jax.experimental.pallas import tpu as pltpu
from jax.sharding import PartitionSpec as P

NP = 2048
FIELDS = 5
AX = 16
ROWS = 64
LANES = 128
TILES = 16
MESH = pl.DeviceIdType.MESH
f32 = jnp.float32
bf16 = jnp.bfloat16

time_step = 0.5
damping = 1.0 / 32.0


def transform_tables():
    q = np.arange(LANES)
    w = 2.0 * np.pi / LANES

    def cas(m):
        angle = w * (m % LANES)
        return np.cos(angle) + np.sin(angle)

    first, second = np.outer(q, q), np.outer(q, q + 1)
    table = np.block([[cas(first), cas(second)], [-cas(-first), cas(-second)]])

    def parts(array):
        array = array.astype(np.float32)
        high = array.astype(ml_dtypes.bfloat16)
        low = (array - high.astype(np.float32)).astype(ml_dtypes.bfloat16)
        return np.stack([high, low])

    psi = 2.0 * np.pi * np.outer(np.arange(9), q) / NP
    twiddle = np.stack([np.cos(psi), np.sin(psi)]).astype(np.float32)
    return parts(table), parts(table.T / NP), twiddle[:, :, None, :]


def cosine(m):
    return math.cos(2.0 * math.pi * (m % 16) / 16)


def sine(m):
    return math.sin(2.0 * math.pi * (m % 16) / 16)


def weighted(terms):
    total = None
    for weight, value in terms:
        if abs(weight) < 1e-9:
            continue
        if abs(weight - 1.0) < 1e-9:
            total = value if total is None else total + value
        elif abs(weight + 1.0) < 1e-9:
            total = -value if total is None else total - value
        else:
            total = weight * value if total is None else total + weight * value
    return total


def forward_16(x):
    e = [None] + [x[p] + x[16 - p] for p in range(1, 8)]
    o = [None] + [x[p] - x[16 - p] for p in range(1, 8)]
    x_even, x_odd = x[0] + x[8], x[0] - x[8]
    ee = [None] + [e[p] + e[8 - p] for p in range(1, 4)]
    eo = [None] + [e[p] - e[8 - p] for p in range(1, 4)]
    oo = [None] + [o[p] + o[8 - p] for p in range(1, 4)]
    oe = [None] + [o[p] - o[8 - p] for p in range(1, 4)]
    cs, ss = [], []
    for c in range(9):
        if c % 2 == 0:
            cs.append(weighted([(1.0, x_even), (cosine(4 * c), e[4])] + [(cosine(p * c), ee[p]) for p in range(1, 4)]))
            ss.append(weighted([(sine(p * c), oe[p]) for p in range(1, 4)]) if 0 < c < 8 else None)
        else:
            cs.append(weighted([(1.0, x_odd)] + [(cosine(p * c), eo[p]) for p in range(1, 4)]))
            ss.append(weighted([(sine(4 * c), o[4])] + [(sine(p * c), oo[p]) for p in range(1, 4)]))
    return cs, ss


def inverse_16(cs, ss):
    x = [None] * 16
    x[0] = weighted([(1.0, v) for v in cs])
    x[8] = weighted([((-1.0) ** c, v) for c, v in enumerate(cs)])
    for p in range(1, 5):
        ev = weighted([(1.0, cs[0]), (cosine(8 * p), cs[8])] + [(cosine(p * c), cs[c]) for c in range(2, 8, 2)])
        eo = weighted([(cosine(p * c), cs[c]) for c in range(1, 8, 2)])
        ov = weighted([(sine(p * c), ss[c]) for c in range(2, 8, 2)])
        oo = weighted([(sine(p * c), ss[c]) for c in range(1, 8, 2)])
        if p == 4:
            x[4], x[12] = ev + oo, ev - oo
            continue
        x[p] = (ev + eo) + (ov + oo)
        x[16 - p] = (ev + eo) - (ov + oo)
        x[8 - p] = (ev - eo) + (oo - ov)
        x[8 + p] = (ev - eo) - (oo - ov)
    return x


def split_dot(values, table_ref):
    high = values.astype(bf16)
    low = (values - high.astype(f32)).astype(bf16)

    def dot(left, right):
        return jnp.dot(left, right, preferred_element_type=f32)

    return dot(high, table_ref[0]) + dot(low, table_ref[0]) + dot(high, table_ref[1])


def interface_kernel(
    off_ref, st_ref, ro_ref, blend_ref, table_ref, back_ref, twiddle_ref,
    ghost_ref, pitch_ref, span_ref,
    state, planes, spectrum, blends, turned, outgoing, pitch_pack, span_pack,
    load_sem, own_sem, row_send, row_recv, back_send, back_recv, halo_send, halo_recv,
):
    me = lax.axis_index("pitch")
    span = lax.axis_index("span")
    left, right = lax.rem(me + 15, 16), lax.rem(me + 1, 16)
    below, above = lax.rem(span + 7, 8), lax.rem(span + 1, 8)
    states = (st_ref, ro_ref)

    def load(s, f):
        return pltpu.make_async_copy(states[s].at[f], state.at[s, f], load_sem.at[s, f])

    def row_block(s, target):
        layer, block = target // 8, target % 8
        axial = 15 - layer if s == 0 else layer
        rows = pl.ds(pl.multiple_of(8 * block, 8), 8)
        return states[s].at[:, axial, rows, :]

    def own_rows(s):
        return pltpu.make_async_copy(row_block(s, me), planes.at[s, me], own_sem.at[s])

    for s in range(2):
        own_rows(s).start()
    for s in range(2):
        for f in range(FIELDS):
            load(s, f).start()

    barrier = pltpu.get_barrier_semaphore()

    def greet(j, carry):
        pl.semaphore_signal(barrier, inc=1, device_id={"pitch": lax.rem(me + j, 16)}, device_id_type=MESH)
        return carry

    lax.fori_loop(1, 16, greet, 0)
    for other in (below, above):
        pl.semaphore_signal(barrier, inc=1, device_id={"span": other}, device_id_type=MESH)
    pl.semaphore_wait(barrier, 17)

    def row_copy(s, target, source):
        return pltpu.make_async_remote_copy(
            src_ref=row_block(s, target), dst_ref=planes.at[s, source],
            send_sem=row_send.at[s, target], recv_sem=row_recv.at[s, source],
            device_id={"pitch": target}, device_id_type=MESH,
        )

    def send_rows(j, carry):
        target = lax.rem(me + j, 16)
        for s in range(2):
            row_copy(s, target, me).start()
        return carry

    lax.fori_loop(1, 16, send_rows, 0)

    def halo_copy(slot, src, dst, where):
        return pltpu.make_async_remote_copy(
            src_ref=src, dst_ref=dst, send_sem=halo_send.at[slot], recv_sem=halo_recv.at[slot],
            device_id=where, device_id_type=MESH,
        )

    halos = (
        halo_copy(0, span_pack.at[0], span_ref.at[0], {"span": above}),
        halo_copy(1, span_pack.at[1], span_ref.at[1], {"span": below}),
        halo_copy(2, pitch_pack, pitch_ref.at[0], {"pitch": right}),
        halo_copy(3, pitch_pack, pitch_ref.at[1], {"pitch": left}),
    )

    lane = lax.broadcasted_iota(jnp.int32, (8, LANES), 1)
    row = lax.broadcasted_iota(jnp.int32, (8, LANES), 0)
    for s in range(2):
        for f in range(FIELDS):
            load(s, f).wait()

        def pack(m, carry):
            f, first = m // 4, 4 * (m % 4)
            edge = jnp.zeros((8, LANES), f32)
            low = jnp.zeros((8, LANES), f32)
            high = jnp.zeros((8, LANES), f32)
            for j in range(4):
                for t in range(8):
                    n = 8 * j + t
                    value = state[s, f, first + j, 8 * t:8 * t + 8, :]
                    edge = jnp.where(lane // 4 == n, pltpu.roll(value, (2 + 4 * n) % LANES, 1), edge)
                    if t == 0:
                        low = jnp.where(row // 2 == j, pltpu.roll(value, 2 * j, 0) if j else value, low)
                    if t == 7:
                        shift = (2 * j + 2) % 8
                        high = jnp.where(row // 2 == j, pltpu.roll(value, shift, 0) if shift else value, high)
            pitch_pack[s, m] = edge
            span_pack[0, s, m] = high
            span_pack[1, s, m] = low
            return carry

        lax.fori_loop(0, 20, pack, 0)
    for copy in halos:
        copy.start()

    nothing = jnp.zeros((8, LANES), f32)
    for c in range(9):
        for f in range(FIELDS):
            blends[c, f, :, 0:LANES] = jnp.broadcast_to(blend_ref[c, f:f + 1, :], (8, LANES))
            other = jnp.broadcast_to(blend_ref[16 - c, f:f + 1, :], (8, LANES)) if 0 < c < 8 else nothing
            blends[c, f, :, LANES:] = other

    offset = off_ref[0]
    shift, hop = lax.rem(offset, LANES), offset // LANES

    for s in range(2):
        own_rows(s).wait()

    def wait_rows(j, carry):
        source = lax.rem(me + j, 16)
        for s in range(2):
            row_copy(s, source, source).wait_recv()
        return carry

    lax.fori_loop(1, 16, wait_rows, 0)

    def forward(f, carry):
        for t in range(TILES):
            turned[t] = pltpu.roll(planes[1, t, f], shift, 1)
        x = []
        for t in range(TILES):
            near = turned[lax.rem(t + 16 - hop, 16)]
            far = turned[lax.rem(t + 15 - hop, 16)]
            x.append(jnp.where(lane >= shift, near, far) - planes[0, t, f])
        cs, ss = forward_16(x)
        for c in range(9):
            cosines, sines = twiddle_ref[0, c], twiddle_ref[1, c]
            if c == 0:
                real, imaginary = cs[0], nothing
            elif c == 8:
                real, imaginary = cs[8] * cosines, -(cs[8] * sines)
            else:
                real = cs[c] * cosines - ss[c] * sines
                imaginary = -(cs[c] * sines + ss[c] * cosines)
            spectrum[c, f, :, 0:LANES] = real
            spectrum[c, f, :, LANES:] = imaginary
        return carry

    lax.fori_loop(0, FIELDS, forward, 0)
    modes = split_dot(spectrum[...].reshape(9 * 40, 256), table_ref)
    modes = modes * blends[...].reshape(9 * 40, 256)
    spectrum[...] = split_dot(modes, back_ref).reshape(9, FIELDS, 8, 256)

    def inverse(f, carry):
        cs, ss = [], []
        for c in range(9):
            cosines, sines = twiddle_ref[0, c], twiddle_ref[1, c]
            real, imaginary = spectrum[c, f, :, 0:LANES], spectrum[c, f, :, LANES:]
            cs.append(real * cosines - imaginary * sines)
            ss.append(-(real * sines + imaginary * cosines))
        x = inverse_16(cs, ss)
        for t in range(TILES):
            outgoing[t, 0, f] = x[t]
            turned[t] = pltpu.roll(x[t], lax.rem(LANES - shift, LANES), 1)
        for t in range(TILES):
            near = turned[lax.rem(t + hop, 16)]
            far = turned[lax.rem(t + hop + 1, 16)]
            outgoing[t, 1, f] = jnp.where(lane < LANES - shift, near, far)
        return carry

    lax.fori_loop(0, FIELDS, inverse, 0)

    def back_copy(target, source):
        return pltpu.make_async_remote_copy(
            src_ref=outgoing.at[target], dst_ref=ghost_ref.at[source],
            send_sem=back_send.at[target], recv_sem=back_recv.at[source],
            device_id={"pitch": target}, device_id_type=MESH,
        )

    def send_back(j, carry):
        back_copy(lax.rem(me + j, 16), me).start()
        return carry

    lax.fori_loop(1, 16, send_back, 0)
    own_back = pltpu.make_async_copy(outgoing.at[me], ghost_ref.at[me], own_sem.at[0])
    own_back.start()
    for copy in halos:
        copy.wait()
    own_back.wait()

    def finish(j, carry):
        other = lax.rem(me + j, 16)
        for s in range(2):
            row_copy(s, other, me).wait_send()
        back_copy(other, me).wait_send()
        back_copy(other, other).wait_recv()
        return carry

    lax.fori_loop(1, 16, finish, 0)


def interface(offset, stator, rotor, blend):
    forward_table, back_table, twiddle = transform_tables()
    whole = pl.BlockSpec(memory_space=pltpu.VMEM)
    anywhere = pl.BlockSpec(memory_space=pl.ANY)
    dma = pltpu.SemaphoreType.DMA
    return pl.pallas_call(
        interface_kernel,
        name="interface",
        out_shape=(
            jax.ShapeDtypeStruct((16, 2, FIELDS, 8, LANES), f32),
            jax.ShapeDtypeStruct((2, 2, 20, 8, LANES), f32),
            jax.ShapeDtypeStruct((2, 2, 20, 8, LANES), f32),
        ),
        in_specs=[pl.BlockSpec(memory_space=pltpu.SMEM), anywhere, anywhere, whole, whole, whole, whole],
        out_specs=(anywhere, anywhere, anywhere),
        scratch_shapes=[
            pltpu.VMEM((2, FIELDS, AX, ROWS, LANES), f32),
            pltpu.VMEM((2, 16, FIELDS, 8, LANES), f32),
            pltpu.VMEM((9, FIELDS, 8, 256), f32),
            pltpu.VMEM((9, FIELDS, 8, 256), f32),
            pltpu.VMEM((16, 8, LANES), f32),
            pltpu.VMEM((16, 2, FIELDS, 8, LANES), f32),
            pltpu.VMEM((2, 20, 8, LANES), f32),
            pltpu.VMEM((2, 2, 20, 8, LANES), f32),
            dma((2, FIELDS)), dma((2,)), dma((2, 16)), dma((2, 16)), dma((16,)), dma((16,)), dma((4,)), dma((4,)),
        ],
        compiler_params=pltpu.CompilerParams(
            collective_id=0, has_side_effects=True, vmem_limit_bytes=48 << 20
        ),
    )(offset, stator, rotor, blend, forward_table, back_table, twiddle)


def update_kernel(
    jac_ref, mix_ref, st_ref, ro_ref, ghost_ref, pitch_ref, span_ref,
    st_out, ro_out,
    cells, result, ghosts, edges, rims, weights,
    load_sem, small_sem, store_sem,
):
    span = lax.axis_index("span")
    states, outs = (st_ref, ro_ref), (st_out, ro_out)

    def load(s, f):
        return pltpu.make_async_copy(states[s].at[f], cells.at[s, f, pl.ds(2, AX), pl.ds(8, ROWS)], load_sem.at[s, f])

    small = (
        pltpu.make_async_copy(pitch_ref, edges, small_sem.at[0]),
        pltpu.make_async_copy(span_ref, rims, small_sem.at[1]),
        pltpu.make_async_copy(ghost_ref, ghosts, small_sem.at[2]),
    )
    for copy in small:
        copy.start()
    for s in range(2):
        for f in range(FIELDS):
            load(s, f).start()

    for d in range(3):
        for f in range(FIELDS):
            for g in range(FIELDS):
                weights[(d * FIELDS + g) * FIELDS + f] = jnp.full((8, LANES), -0.5 * time_step * jac_ref[d, f, g], f32)
    for f in range(FIELDS):
        for t in range(8):
            for a in range(2):
                cells[0, f, a, 8 + 8 * t:16 + 8 * t, :] = jnp.zeros((8, LANES), f32)
                cells[1, f, 18 + a, 8 + 8 * t:16 + 8 * t, :] = jnp.zeros((8, LANES), f32)
    for copy in small:
        copy.wait()
    lane = lax.broadcasted_iota(jnp.int32, (8, LANES), 1)
    keep_low = jnp.where(span == 0, 0.0, 1.0).astype(f32)
    keep_high = jnp.where(span == 7, 0.0, 1.0).astype(f32)
    for s in range(2):

        def unpack(m, carry):
            f, first = m // 4, 4 * (m % 4)
            low = rims[0, s, m] * keep_low
            high = rims[1, s, m] * keep_high
            for j in range(4):
                cells[s, f, 2 + first + j, 6:8, :] = low[2 * j:2 * j + 2, :]
                cells[s, f, 2 + first + j, 72:74, :] = high[2 * j:2 * j + 2, :]
            edges[0, s, m] = jnp.where(lane % 4 < 2, edges[0, s, m], edges[1, s, m])
            return carry

        lax.fori_loop(0, 20, unpack, 0)

    for s in range(2):
        for f in range(FIELDS):
            load(s, f).wait()

        def fill(block, carry):
            rows = pl.ds(pl.multiple_of(8 + 8 * block, 8), 8)
            for layer in range(2):
                planes = []
                for g in range(FIELDS):
                    change = ghosts[8 * layer + block, s, g]
                    planes.append(cells[s, g, 17 - layer if s == 0 else 2 + layer, rows, :] + (change if s == 0 else -change))
                for f in range(FIELDS):
                    total = mix_ref[f, 0] * planes[0]
                    for g in range(1, FIELDS):
                        total = total + mix_ref[f, g] * planes[g]
                    cells[s, f, 18 + layer if s == 0 else 1 - layer, rows, :] = total
            return carry

        lax.fori_loop(0, 8, fill, 0)

        def store(a):
            return pltpu.make_async_copy(result.at[s, :, a], outs[s].at[:, a], store_sem.at[s, a])

        def layer_update(a, carry):
            for half in range(2):
                start = 8 + 32 * half
                sums = []
                slopes = []
                for g in range(FIELDS):

                    def get(axial, radial):
                        return cells[s, g, a + 2 + axial, start + radial:start + radial + 32, :].reshape(4, 8, LANES)

                    centre = get(0, 0)
                    pack = edges[0, s, 4 * g + a // 4]
                    base = 126 - 32 * lax.rem(a, 4)
                    halo = jnp.stack([
                        pltpu.roll(pack, lax.rem(base - 4 * (4 * half + t) + 2 * LANES, LANES), 1) for t in range(4)
                    ])
                    right_1 = pltpu.roll(jnp.where(lane == 0, halo, centre), LANES - 1, 2)
                    right_2 = pltpu.roll(jnp.where(lane < 2, halo, centre), LANES - 2, 2)
                    left_1 = pltpu.roll(jnp.where(lane == LANES - 1, halo, centre), 1, 2)
                    left_2 = pltpu.roll(jnp.where(lane >= LANES - 2, halo, centre), 2, 2)
                    ahead, behind = get(1, 0), get(-1, 0)
                    up, down = get(0, 1), get(0, -1)
                    near = (ahead + behind) + (up + down) + (right_1 + left_1)
                    far = (get(2, 0) + get(-2, 0)) + (get(0, 2) + get(0, -2)) + (right_2 + left_2)
                    scale = time_step * damping
                    sums.append((1.0 - 18.0 * scale) * centre + (4.0 * scale) * near - scale * far)
                    slopes.append((ahead - behind, up - down, right_1 - left_1))
                for d in range(3):
                    for g in range(FIELDS):
                        for f in range(FIELDS):
                            sums[f] = sums[f] + weights[(d * FIELDS + g) * FIELDS + f] * slopes[g][d]
                for f in range(FIELDS):
                    result[s, f, a, 32 * half:32 * half + 32, :] = sums[f].reshape(32, LANES)
            store(a).start()
            return carry

        lax.fori_loop(0, AX, layer_update, 0)

    for s in range(2):
        for a in range(AX):
            pltpu.make_async_copy(result.at[s, :, a], outs[s].at[:, a], store_sem.at[s, a]).wait()


def update(jacobians, field_mix, stator, rotor, ghosts, pitch_halo, span_halo):
    anywhere = pl.BlockSpec(memory_space=pl.ANY)
    scalars = pl.BlockSpec(memory_space=pltpu.SMEM)
    dma = pltpu.SemaphoreType.DMA
    shape = jax.ShapeDtypeStruct((FIELDS, AX, ROWS, LANES), f32)
    return pl.pallas_call(
        update_kernel,
        name="update",
        out_shape=(shape, shape),
        in_specs=[scalars, scalars] + [anywhere] * 5,
        out_specs=(anywhere, anywhere),
        scratch_shapes=[
            pltpu.VMEM((2, FIELDS, AX + 4, ROWS + 16, LANES), f32),
            pltpu.VMEM((2, FIELDS, AX, ROWS, LANES), f32),
            pltpu.VMEM((16, 2, FIELDS, 8, LANES), f32),
            pltpu.VMEM((2, 2, 20, 8, LANES), f32),
            pltpu.VMEM((2, 2, 20, 8, LANES), f32),
            pltpu.VMEM((75, 8, LANES), f32),
            dma((2, FIELDS)), dma((3,)), dma((2, AX)),
        ],
        compiler_params=pltpu.CompilerParams(vmem_limit_bytes=48 << 20),
    )(jacobians, field_mix, stator, rotor, ghosts, pitch_halo, span_halo)


def shards(stator_state, rotor_state, jacobians, field_mix, mode_blend, rotor_offset):
    blend = mode_blend.reshape(FIELDS, LANES, 16).transpose(2, 0, 1)
    ghosts, pitch_halo, span_halo = interface(rotor_offset, stator_state, rotor_state, blend)
    return update(jacobians, field_mix, stator_state, rotor_state, ghosts, pitch_halo, span_halo)


def solution(mesh):
    in_specs = (P(None, None, "span", "pitch"), P(None, None, "span", "pitch"), P(), P(), P(), P())
    out_specs = (P(None, None, "span", "pitch"), P(None, None, "span", "pitch"))
    return jax.shard_map(shards, mesh=mesh, in_specs=in_specs, out_specs=out_specs, check_vma=False)
```

time: 494 us -> 60.7 us (0.12)
  the two profiles are of different devices: /device:TPU:1 before, /device:TPU:0 now
where the time goes in v1:
time: 60.7 us; the launch traced here: 60.3 us
  Pallas kernels  52.8 us (87%)
  local copies, waits for them, and re-layouts  6.19 us (10%)
  between operations  1.31 us (2%)
    pallas_call x1, Pallas kernels, interface(): pl.pallas_call(interface_kernel, name='interface', out_shape=(jax.ShapeDt...  29.3 us
    pallas_call x1, Pallas kernels, update(): pl.pallas_call(update_kernel, name='update', out_shape=(shape, shape), in...  23.5 us
    unnamed x11, local copies, waits for them, and re-layouts  5.05 us

profile of v1, /device:TPU:0, one launch (start us, length us, event | category | flops | bytes accessed | tf_op | source)
XLA Modules:
  0.0 60.3 jit_solution(5927153682264477489)
XLA Ops:
  1.3 0.7 %copy.13.jac_ref = f32[3,5,5]{2,1,0:T(8,128)S(1)} copy(f32[3,5,5]{2,0,1:T(4,128)} %param.11) | data formatting | bytes 600 | tf_op args[2]
  2.0 1.0 %reshape.7 = f32[5,128,16]{2,1,0:T(8,128)S(1)} reshape(f32[5,2048]{1,0:T(8,128)} %param.13) | data formatting | bytes 81920 | tf_op jit(solution)/shard_map/reshape | solution.py:487
  3.0 0.2 copy.12
  3.1 0.0 copy-start
  3.1 1.7 %copy-done = f32[5,16,64,128]{3,2,1,0:T(8,128)S(1)} copy-done((f32[5,16,64,128]{3,2,1,0:T(8,128)S(1)}, f32[5,16,64,128]{3,2,1,0:T(8,128)}, u32[]{:S(2)}) %copy-start) | copy-done | bytes 2621464
  4.9 0.0 copy-start.1
  4.9 0.9 %copy-done.1 = bf16[2,256,256]{2,1,0:T(8,128)(2,1)S(1)} copy-done((bf16[2,256,256]{2,1,0:T(8,128)(2,1)S(1)}, bf16[2,256,256]{2,1,0:T(8,128)(2,1)}, u32[]{:S(2)}) %copy-start.1) | copy-done | bytes 262168
  5.8 0.0 copy-start.2
  5.8 0.9 %copy-done.2 = bf16[2,256,256]{2,1,0:T(8,128)(2,1)S(1)} copy-done((bf16[2,256,256]{2,1,0:T(8,128)(2,1)S(1)}, bf16[2,256,256]{2,1,0:T(8,128)(2,1)}, u32[]{:S(2)}) %copy-start.2) | copy-done | bytes 262168
  6.8 0.0 copy-start.3
  6.8 0.7 %copy-done.3 = f32[2,9,1,128]{3,2,1,0:T(1,128)S(1)} copy-done((f32[2,9,1,128]{3,2,1,0:T(1,128)S(1)}, f32[2,9,1,128]{3,2,1,0:T(1,128)}, u32[]{:S(2)}) %copy-start.3) | copy-done | bytes 9240
  7.5 0.0 copy-start.4
  7.5 29.3 %interface.1 = (f32[16,2,5,8,128]{4,3,2,1,0:T(8,128)S(1)}, f32[2,2,20,8,128]{4,3,2,1,0:T(8,128)S(1)}, f32[2,2,20,8,128]{4,3,2,1,0:T(8,128)S(1)}) custom-call(s32[1]{0:T(128)S(6)} %copy.14.off_ref, f32[5,16,64,128]{3,2,1,0:T(8,128)S(1)} %copy-done, f32[5,16,64,128]{3,2,1,0:T(8,128)} %ro_ref.3, f32[16,5,128]{2,1,0:T(8,128)S(1)} %bitcast.1, ...), custom_call_target="tpu_custom_call" | custom-call | tf_op jit(solution)/shard_map/interface/pallas_call | solution.py:318
  36.8 0.0 copy-done.4
  36.8 23.5 %update.1 = (f32[5,16,64,128]{3,2,1,0:T(8,128)}, f32[5,16,64,128]{3,2,1,0:T(8,128)}) custom-call(f32[3,5,5]{2,1,0:T(8,128)S(1)} %copy.13.jac_ref, f32[5,5]{1,0:T(8,128)S(1)} %copy-done.4, f32[5,16,64,128]{3,2,1,0:T(8,128)S(1)} %copy-done, f32[5,16,64,128]{3,2,1,0:T(8,128)} %ro_ref.3, f32[16,2,5,8,128]{4,3,2,1,0:T(8,128)S(1)} %get-tuple-element.5.ghost_ref, ...), custom_call_target="tpu_custom_call" | custom-call | tf_op jit(solution)/shard_map/update/pallas_call | solution.py:467
Async XLA Ops:
  3.1 1.8 %copy-start = (f32[5,16,64,128]{3,2,1,0:T(8,128)S(1)}, f32[5,16,64,128]{3,2,1,0:T(8,128)}, u32[]{:S(2)}) copy-start(f32[5,16,64,128]{3,2,1,0:T(8,128)} %st_ref.3) | copy-start | bytes 7864324
  4.9 0.9 %copy-start.1 = (bf16[2,256,256]{2,1,0:T(8,128)(2,1)S(1)}, bf16[2,256,256]{2,1,0:T(8,128)(2,1)}, u32[]{:S(2)}) copy-start(bf16[2,256,256]{2,1,0:T(8,128)(2,1)} %constant.7.clone.back_ref) | copy-start | bytes 786436
  5.8 0.9 %copy-start.2 = (bf16[2,256,256]{2,1,0:T(8,128)(2,1)S(1)}, bf16[2,256,256]{2,1,0:T(8,128)(2,1)}, u32[]{:S(2)}) copy-start(bf16[2,256,256]{2,1,0:T(8,128)(2,1)} %constant.6.clone.table_ref) | copy-start | bytes 786436
  6.8 0.7 %copy-start.3 = (f32[2,9,1,128]{3,2,1,0:T(1,128)S(1)}, f32[2,9,1,128]{3,2,1,0:T(1,128)}, u32[]{:S(2)}) copy-start(f32[2,9,1,128]{3,2,1,0:T(1,128)} %constant.8.clone.twiddle_ref) | copy-start | bytes 27652
  7.5 29.3 %copy-start.4 = (f32[5,5]{1,0:T(8,128)S(1)}, f32[5,5]{1,0:T(8,128)}, u32[]{:S(2)}) copy-start(f32[5,5]{1,0:T(8,128)} %mix_ref.1) | copy-start | bytes 304

commit v2 on v1

v2 whole, which is shorter than its diff:
```python
import math

import jax
import jax.numpy as jnp
import ml_dtypes
import numpy as np
from jax import lax
from jax.experimental import pallas as pl
from jax.experimental.pallas import tpu as pltpu
from jax.sharding import PartitionSpec as P

NP = 2048
FIELDS = 5
AX = 16
ROWS = 64
LANES = 128
TILES = 16
MESH = pl.DeviceIdType.MESH
f32 = jnp.float32
bf16 = jnp.bfloat16

time_step = 0.5
damping = 1.0 / 32.0


def transform_tables():
    q = np.arange(LANES)
    w = 2.0 * np.pi / LANES

    def cas(m):
        angle = w * (m % LANES)
        return np.cos(angle) + np.sin(angle)

    first, second = np.outer(q, q), np.outer(q, q + 1)
    table = np.block([[cas(first), cas(second)], [-cas(-first), cas(-second)]])

    def parts(array):
        array = array.astype(np.float32)
        high = array.astype(ml_dtypes.bfloat16)
        low = (array - high.astype(np.float32)).astype(ml_dtypes.bfloat16)
        return np.stack([high, low])

    psi = 2.0 * np.pi * np.outer(np.arange(9), q) / NP
    twiddle = np.stack([np.cos(psi), np.sin(psi)]).astype(np.float32)
    return parts(table), parts(table.T / NP), twiddle[:, :, None, :]


def cosine(m):
    return math.cos(2.0 * math.pi * (m % 16) / 16)


def sine(m):
    return math.sin(2.0 * math.pi * (m % 16) / 16)


def weighted(terms):
    total = None
    for weight, value in terms:
        if abs(weight) < 1e-9:
            continue
        if abs(weight - 1.0) < 1e-9:
            total = value if total is None else total + value
        elif abs(weight + 1.0) < 1e-9:
            total = -value if total is None else total - value
        else:
            total = weight * value if total is None else total + weight * value
    return total


def forward_16(x):
    e = [None] + [x[p] + x[16 - p] for p in range(1, 8)]
    o = [None] + [x[p] - x[16 - p] for p in range(1, 8)]
    x_even, x_odd = x[0] + x[8], x[0] - x[8]
    ee = [None] + [e[p] + e[8 - p] for p in range(1, 4)]
    eo = [None] + [e[p] - e[8 - p] for p in range(1, 4)]
    oo = [None] + [o[p] + o[8 - p] for p in range(1, 4)]
    oe = [None] + [o[p] - o[8 - p] for p in range(1, 4)]
    cs, ss = [], []
    for c in range(9):
        if c % 2 == 0:
            cs.append(weighted([(1.0, x_even), (cosine(4 * c), e[4])] + [(cosine(p * c), ee[p]) for p in range(1, 4)]))
            ss.append(weighted([(sine(p * c), oe[p]) for p in range(1, 4)]) if 0 < c < 8 else None)
        else:
            cs.append(weighted([(1.0, x_odd)] + [(cosine(p * c), eo[p]) for p in range(1, 4)]))
            ss.append(weighted([(sine(4 * c), o[4])] + [(sine(p * c), oo[p]) for p in range(1, 4)]))
    return cs, ss


def inverse_16(cs, ss):
    x = [None] * 16
    x[0] = weighted([(1.0, v) for v in cs])
    x[8] = weighted([((-1.0) ** c, v) for c, v in enumerate(cs)])
    for p in range(1, 5):
        ev = weighted([(1.0, cs[0]), (cosine(8 * p), cs[8])] + [(cosine(p * c), cs[c]) for c in range(2, 8, 2)])
        eo = weighted([(cosine(p * c), cs[c]) for c in range(1, 8, 2)])
        ov = weighted([(sine(p * c), ss[c]) for c in range(2, 8, 2)])
        oo = weighted([(sine(p * c), ss[c]) for c in range(1, 8, 2)])
        if p == 4:
            x[4], x[12] = ev + oo, ev - oo
            continue
        x[p] = (ev + eo) + (ov + oo)
        x[16 - p] = (ev + eo) - (ov + oo)
        x[8 - p] = (ev - eo) + (oo - ov)
        x[8 + p] = (ev - eo) - (oo - ov)
    return x


def split_dot(values, table_ref):
    high = values.astype(bf16)
    low = (values - high.astype(f32)).astype(bf16)

    def dot(left, right):
        return jnp.dot(left, right, preferred_element_type=f32)

    return dot(high, table_ref[0]) + dot(low, table_ref[0]) + dot(high, table_ref[1])


def section_kernel(
    off_ref, st_ref, ro_ref, blend_hbm, jac_hbm, mix_hbm, table_hbm, back_hbm, twiddle_hbm, band_hbm,
    partial, ghost_ref, weights, mixes,
    cells, planes, spectrum, blends, turned, outgoing, pitch_pack, pitch_recv, span_pack, span_recv,
    bent_a, bent_b, edge_fix, permuted, blend_v, jac_v, mix_v, table_ref, back_ref, twiddle_ref, band_ref,
    load_sem, own_sem, row_send, row_recv, back_send, back_recv, halo_send, halo_recv, small_sem,
):
    me = lax.axis_index("pitch")
    span = lax.axis_index("span")
    left, right = lax.rem(me + 15, 16), lax.rem(me + 1, 16)
    below, above = lax.rem(span + 7, 8), lax.rem(span + 1, 8)
    states = (st_ref, ro_ref)

    def load(s, f):
        return pltpu.make_async_copy(states[s].at[f], cells.at[s, f, pl.ds(2, AX), pl.ds(8, ROWS)], load_sem.at[s, f])

    def row_block(s, target):
        layer, block = target // 8, target % 8
        axial = 15 - layer if s == 0 else layer
        rows = pl.ds(pl.multiple_of(8 * block, 8), 8)
        return states[s].at[:, axial, rows, :]

    def own_rows(s):
        return pltpu.make_async_copy(row_block(s, me), planes.at[s, me], own_sem.at[s])

    barrier = pltpu.get_barrier_semaphore()

    def greet(j, carry):
        pl.semaphore_signal(barrier, inc=1, device_id={"pitch": lax.rem(me + j, 16)}, device_id_type=MESH)
        return carry

    lax.fori_loop(1, 16, greet, 0)
    for other in (below, above):
        pl.semaphore_signal(barrier, inc=1, device_id={"span": other}, device_id_type=MESH)

    smalls = [
        pltpu.make_async_copy(source, target, small_sem.at[i])
        for i, (source, target) in enumerate((
            (blend_hbm, blend_v), (jac_hbm, jac_v), (mix_hbm, mix_v),
            (table_hbm, table_ref), (back_hbm, back_ref), (twiddle_hbm, twiddle_ref), (band_hbm, band_ref),
        ))
    ]
    for s in range(2):
        own_rows(s).start()
    for s in range(2):
        for f in range(FIELDS):
            load(s, f).start()
    for copy in smalls:
        copy.start()

    lane = lax.broadcasted_iota(jnp.int32, (8, LANES), 1)
    row = lax.broadcasted_iota(jnp.int32, (8, LANES), 0)
    group = lane % 4
    nothing = jnp.zeros((8, LANES), f32)
    for s in range(2):
        for f in range(FIELDS):
            for t in range(8):
                for a in (0, 1, 18, 19):
                    cells[s, f, a, 8 + 8 * t:16 + 8 * t, :] = nothing

    pl.semaphore_wait(barrier, 17)

    def row_copy(s, target, source):
        return pltpu.make_async_remote_copy(
            src_ref=row_block(s, target), dst_ref=planes.at[s, source],
            send_sem=row_send.at[s, target], recv_sem=row_recv.at[s, source],
            device_id={"pitch": target}, device_id_type=MESH,
        )

    def send_rows(j, carry):
        target = lax.rem(me + j, 16)
        for s in range(2):
            row_copy(s, target, me).start()
        return carry

    lax.fori_loop(1, 16, send_rows, 0)

    def halo_copy(slot, src, dst, where):
        return pltpu.make_async_remote_copy(
            src_ref=src, dst_ref=dst, send_sem=halo_send.at[slot], recv_sem=halo_recv.at[slot],
            device_id=where, device_id_type=MESH,
        )

    to_above = halo_copy(0, span_pack.at[0], span_recv.at[0], {"span": above})
    to_below = halo_copy(1, span_pack.at[1], span_recv.at[1], {"span": below})
    to_right = halo_copy(2, pitch_pack.at[0], pitch_recv.at[0], {"pitch": right})
    to_left = halo_copy(3, pitch_pack.at[1], pitch_recv.at[1], {"pitch": left})

    for s in range(2):
        for f in range(FIELDS):
            load(s, f).wait()

        def pack(pair, carry):
            found = []
            for half in range(2):
                m = 2 * pair + half
                f, first = m // 4, 2 + 4 * (m % 4)
                edge = jnp.zeros((8, LANES), f32)
                low = jnp.zeros((8, LANES), f32)
                high = jnp.zeros((8, LANES), f32)
                for j in range(4):
                    for t in range(8):
                        n = 8 * j + t
                        value = cells[s, f, first + j, 8 + 8 * t:16 + 8 * t, :]
                        edge = jnp.where(lane // 4 == n, pltpu.roll(value, (2 + 4 * n) % LANES, 1), edge)
                        if t == 0:
                            low = jnp.where(row // 2 == j, pltpu.roll(value, 2 * j, 0) if j else value, low)
                        if t == 7:
                            shift = (2 * j + 2) % 8
                            high = jnp.where(row // 2 == j, pltpu.roll(value, shift, 0) if shift else value, high)
                span_pack[0, s, m] = high
                span_pack[1, s, m] = low
                found.append(edge)
            pitch_pack[0, s, pair] = jnp.where(group < 2, found[0], pltpu.roll(found[1], 2, 1))
            pitch_pack[1, s, pair] = jnp.where(group < 2, pltpu.roll(found[0], LANES - 2, 1), found[1])
            return carry

        lax.fori_loop(0, 10, pack, 0)
    for copy in (to_above, to_below, to_right, to_left):
        copy.start()

    for copy in smalls:
        copy.wait()
    for d in range(3):
        for f in range(FIELDS):
            for g in range(FIELDS):
                value = jnp.broadcast_to(jac_v[f, d:d + 1, g:g + 1], (8, LANES))
                weights[(d * FIELDS + g) * FIELDS + f] = (-0.5 * time_step) * value
    for f in range(FIELDS):
        for g in range(FIELDS):
            mixes[f * FIELDS + g] = jnp.broadcast_to(mix_v[f:f + 1, g:g + 1], (8, LANES))

    spare = jnp.zeros((3, LANES), f32)
    blend_rows = jnp.concatenate(
        [part for t in range(TILES) for part in (blend_v[:, LANES * t:LANES * t + LANES], spare)], axis=0
    )
    source_lane = lax.broadcasted_iota(jnp.int32, (LANES, LANES), 0)
    target_lane = lax.broadcasted_iota(jnp.int32, (LANES, LANES), 1)
    chosen = (8 * (source_lane % 16) + source_lane // 16 == target_lane).astype(f32)
    permuted[...] = jnp.dot(
        blend_rows, chosen, precision=lax.Precision.HIGHEST, preferred_element_type=f32
    ).reshape(TILES, 8, LANES)

    def mode_row(k):
        total = nothing
        for t in range(TILES):
            shift = (8 * (t - k)) % LANES
            value = permuted[t]
            total = jnp.where(lane // 8 == t, pltpu.roll(value, shift, 1) if shift else value, total)
        return total

    for c in range(9):
        near = mode_row(c)
        other = mode_row(16 - c) if 0 < c < 8 else nothing
        for f in range(FIELDS):
            blends[c, f, :, 0:LANES] = jnp.broadcast_to(near[f:f + 1, :], (8, LANES))
            blends[c, f, :, LANES:] = jnp.broadcast_to(other[f:f + 1, :], (8, LANES))

    def base_ghosts(block, carry):
        rows = pl.ds(pl.multiple_of(8 + 8 * block, 8), 8)
        for s in range(2):
            for layer in range(2):
                kept = [cells[s, g, 17 - layer if s == 0 else 2 + layer, rows, :] for g in range(FIELDS)]
                for f in range(FIELDS):
                    total = mixes[f * FIELDS] * kept[0]
                    for g in range(1, FIELDS):
                        total = total + mixes[f * FIELDS + g] * kept[g]
                    cells[s, f, 18 + layer if s == 0 else 1 - layer, rows, :] = total
        return carry

    lax.fori_loop(0, 8, base_ghosts, 0)

    offset = off_ref[0]
    shift, hop = lax.rem(offset, LANES), offset // LANES

    for s in range(2):
        own_rows(s).wait()

    def wait_rows(j, carry):
        source = lax.rem(me + j, 16)
        for s in range(2):
            row_copy(s, source, source).wait_recv()
        return carry

    lax.fori_loop(1, 16, wait_rows, 0)

    def forward(f, carry):
        for t in range(TILES):
            turned[t] = pltpu.roll(planes[1, t, f], shift, 1)
        x = []
        for t in range(TILES):
            near = turned[lax.rem(t + 16 - hop, 16)]
            far = turned[lax.rem(t + 15 - hop, 16)]
            x.append(jnp.where(lane >= shift, near, far) - planes[0, t, f])
        cs, ss = forward_16(x)
        for c in range(9):
            cosines, sines = twiddle_ref[0, c], twiddle_ref[1, c]
            if c == 0:
                real, imaginary = cs[0], nothing
            elif c == 8:
                real, imaginary = cs[8] * cosines, -(cs[8] * sines)
            else:
                real = cs[c] * cosines - ss[c] * sines
                imaginary = -(cs[c] * sines + ss[c] * cosines)
            spectrum[c, f, :, 0:LANES] = real
            spectrum[c, f, :, LANES:] = imaginary
        return carry

    lax.fori_loop(0, FIELDS, forward, 0)
    modes = split_dot(spectrum[...].reshape(9 * 40, 256), table_ref)
    modes = modes * blends[...].reshape(9 * 40, 256)
    spectrum[...] = split_dot(modes, back_ref).reshape(9, FIELDS, 8, 256)

    def inverse(f, carry):
        cs, ss = [], []
        for c in range(9):
            cosines, sines = twiddle_ref[0, c], twiddle_ref[1, c]
            real, imaginary = spectrum[c, f, :, 0:LANES], spectrum[c, f, :, LANES:]
            cs.append(real * cosines - imaginary * sines)
            ss.append(-(real * sines + imaginary * cosines))
        x = inverse_16(cs, ss)
        for t in range(TILES):
            outgoing[t, 0, f] = x[t]
            turned[t] = pltpu.roll(x[t], lax.rem(LANES - shift, LANES), 1)
        for t in range(TILES):
            near = turned[lax.rem(t + hop, 16)]
            far = turned[lax.rem(t + hop + 1, 16)]
            outgoing[t, 1, f] = jnp.where(lane < LANES - shift, near, far)
        return carry

    lax.fori_loop(0, FIELDS, inverse, 0)

    def back_copy(target, source):
        return pltpu.make_async_remote_copy(
            src_ref=outgoing.at[target], dst_ref=ghost_ref.at[source],
            send_sem=back_send.at[target], recv_sem=back_recv.at[source],
            device_id={"pitch": target}, device_id_type=MESH,
        )

    def send_back(j, carry):
        back_copy(lax.rem(me + j, 16), me).start()
        return carry

    lax.fori_loop(1, 16, send_back, 0)
    own_back = pltpu.make_async_copy(outgoing.at[me], ghost_ref.at[me], own_sem.at[0])
    own_back.start()

    for copy in (to_above, to_below, to_right, to_left):
        copy.wait()
    keep_low = jnp.where(span == 0, 0.0, 1.0).astype(f32)
    keep_high = jnp.where(span == 7, 0.0, 1.0).astype(f32)
    scale = time_step * damping
    for s in range(2):

        def unpack(m, carry):
            f, first = m // 4, 4 * (m % 4)
            low = span_recv[0, s, m] * keep_low
            high = span_recv[1, s, m] * keep_high
            for j in range(4):
                cells[s, f, 2 + first + j, 6:8, :] = low[2 * j:2 * j + 2, :]
                cells[s, f, 2 + first + j, 72:74, :] = high[2 * j:2 * j + 2, :]
            return carry

        lax.fori_loop(0, 20, unpack, 0)

        def edges(quarter_pair, carry):
            total = [[None] * FIELDS, [None] * FIELDS]
            for g in range(FIELDS):
                from_left, from_right = pitch_recv[0, s, 2 * g + quarter_pair], pitch_recv[1, s, 2 * g + quarter_pair]
                for half in range(2):
                    if half == 0:
                        halo = jnp.where(group < 2, from_left, pltpu.roll(from_right, 2, 1))
                    else:
                        halo = jnp.where(group < 2, pltpu.roll(from_left, LANES - 2, 1), from_right)
                    plus_1, minus_1 = pltpu.roll(halo, LANES - 1, 1), pltpu.roll(halo, 1, 1)
                    plus_2, minus_2 = pltpu.roll(halo, LANES - 2, 1), pltpu.roll(halo, 2, 1)
                    slope = jnp.where(group == 1, plus_1, jnp.where(group == 2, -minus_1, 0.0))
                    smooth = jnp.where(group < 2, plus_2, minus_2) - 4.0 * jnp.where(
                        group == 1, plus_1, jnp.where(group == 2, minus_1, 0.0)
                    )
                    for f in range(FIELDS):
                        term = weights[(2 * FIELDS + g) * FIELDS + f] * slope
                        if f == g:
                            term = term - scale * smooth
                        total[half][f] = term if total[half][f] is None else total[half][f] + term
            for half in range(2):
                for f in range(FIELDS):
                    edge_fix[s, f, 2 * quarter_pair + half] = total[half][f]
            return carry

        lax.fori_loop(0, 2, edges, 0)

    rim = (lane < 2) | (lane >= LANES - 2)

    def bend(layer, target):
        s, a = layer // AX, layer % AX
        values = cells[s, :, a + 2, 8:8 + ROWS, :].reshape(FIELDS * ROWS, LANES)
        high = values.astype(bf16)
        low = (values - high.astype(f32)).astype(bf16)
        both = jnp.concatenate([high, low], axis=1)
        target[...] = jnp.dot(both, band_ref[...], preferred_element_type=f32).reshape(FIELDS, ROWS, 256)

    def advance(layer, bent):
        s, a = layer // AX, layer % AX
        for half in range(2):
            start = 8 + 32 * half
            sums = [None] * FIELDS
            for g in range(FIELDS):

                def get(axial, radial):
                    return cells[s, g, a + 2 + axial, start + radial:start + radial + 32, :].reshape(4, 8, LANES)

                ahead, behind = get(1, 0), get(-1, 0)
                up, down = get(0, 1), get(0, -1)
                near = (ahead + behind) + (up + down)
                far = (get(2, 0) + get(-2, 0)) + (get(0, 2) + get(0, -2))
                along = bent[g, 32 * half:32 * half + 32, 0:LANES].reshape(4, 8, LANES)
                own = bent[g, 32 * half:32 * half + 32, LANES:].reshape(4, 8, LANES)
                own = own + ((4.0 * scale) * near - scale * far)
                fix = edge_fix[s, g, a // 4]
                base = 126 - 32 * lax.rem(a, 4)
                own = own + jnp.stack([
                    jnp.where(rim, pltpu.roll(fix, lax.rem(base - 4 * (4 * half + t) + 2 * LANES, LANES), 1), 0.0)
                    for t in range(4)
                ])
                sums[g] = own if sums[g] is None else sums[g] + own
                for d, slope in enumerate((ahead - behind, up - down, along)):
                    for f in range(FIELDS):
                        term = weights[(d * FIELDS + g) * FIELDS + f] * slope
                        sums[f] = term if sums[f] is None else sums[f] + term
            for f in range(FIELDS):
                partial[s, f, a, 32 * half:32 * half + 32, :] = sums[f].reshape(32, LANES)

    bend(0, bent_a)

    def two_layers(i, carry):
        bend(2 * i + 1, bent_b)
        advance(2 * i, bent_a)
        bend(jnp.minimum(2 * i + 2, 2 * AX - 1), bent_a)
        advance(2 * i + 1, bent_b)
        return carry

    lax.fori_loop(0, AX, two_layers, 0)

    own_back.wait()

    def finish(j, carry):
        other = lax.rem(me + j, 16)
        for s in range(2):
            row_copy(s, other, me).wait_send()
        back_copy(other, me).wait_send()
        back_copy(other, other).wait_recv()
        return carry

    lax.fori_loop(1, 16, finish, 0)


def band_table():
    position = np.arange(LANES)
    scale = time_step * damping
    slope = np.zeros((LANES, LANES))
    smooth = np.zeros((LANES, LANES))
    for step, weight in ((1, 1.0), (-1, -1.0)):
        inside = position[(position + step >= 0) & (position + step < LANES)]
        slope[inside + step, inside] += weight
    for step, weight in ((0, 1.0 - 18.0 * scale), (1, 4.0 * scale), (-1, 4.0 * scale), (2, -scale), (-2, -scale)):
        inside = position[(position + step >= 0) & (position + step < LANES)]
        smooth[inside + step, inside] += weight
    table = np.concatenate([slope, smooth], axis=1)
    return np.concatenate([table, table], axis=0).astype(ml_dtypes.bfloat16)


def section(offset, stator, rotor, blend, jacobians, field_mix):
    forward_table, back_table, twiddle = transform_tables()
    whole = pl.BlockSpec(memory_space=pltpu.VMEM)
    anywhere = pl.BlockSpec(memory_space=pl.ANY)
    dma = pltpu.SemaphoreType.DMA
    return pl.pallas_call(
        section_kernel,
        name="section",
        out_shape=(
            pltpu.VMEM((2, FIELDS, AX, ROWS, LANES), f32),
            pltpu.VMEM((16, 2, FIELDS, 8, LANES), f32),
            pltpu.VMEM((75, 8, LANES), f32),
            pltpu.VMEM((25, 8, LANES), f32),
        ),
        in_specs=[pl.BlockSpec(memory_space=pltpu.SMEM)] + [pl.BlockSpec(memory_space=pltpu.HBM)] * 9,
        out_specs=(whole, whole, whole, whole),
        scratch_shapes=[
            pltpu.VMEM((2, FIELDS, AX + 4, ROWS + 16, LANES), f32),
            pltpu.VMEM((2, 16, FIELDS, 8, LANES), f32),
            pltpu.VMEM((9, FIELDS, 8, 256), f32),
            pltpu.VMEM((9, FIELDS, 8, 256), f32),
            pltpu.VMEM((16, 8, LANES), f32),
            pltpu.VMEM((16, 2, FIELDS, 8, LANES), f32),
            pltpu.VMEM((2, 2, 10, 8, LANES), f32),
            pltpu.VMEM((2, 2, 10, 8, LANES), f32),
            pltpu.VMEM((2, 2, 20, 8, LANES), f32),
            pltpu.VMEM((2, 2, 20, 8, LANES), f32),
            pltpu.VMEM((FIELDS, ROWS, 256), f32),
            pltpu.VMEM((FIELDS, ROWS, 256), f32),
            pltpu.VMEM((2, FIELDS, 4, 8, LANES), f32),
            pltpu.VMEM((TILES, 8, LANES), f32),
            pltpu.VMEM((FIELDS, NP), f32),
            pltpu.VMEM((FIELDS, 3, FIELDS), f32),
            pltpu.VMEM((FIELDS, FIELDS), f32),
            pltpu.VMEM((2, 256, 256), bf16),
            pltpu.VMEM((2, 256, 256), bf16),
            pltpu.VMEM((2, 9, 1, LANES), f32),
            pltpu.VMEM((256, 256), bf16),
            dma((2, FIELDS)), dma((2,)), dma((2, 16)), dma((2, 16)), dma((16,)), dma((16,)), dma((4,)), dma((4,)), dma((7,)),
        ],
        compiler_params=pltpu.CompilerParams(
            collective_id=0, has_side_effects=True, vmem_limit_bytes=32 << 20
        ),
    )(offset, *(
        pltpu.with_memory_space_constraint(jnp.asarray(x), pltpu.HBM)
        for x in (
            stator, rotor, blend, jacobians.transpose(1, 0, 2), field_mix,
            forward_table, back_table, twiddle, band_table(),
        )
    ))


def close_kernel(partial, ghosts, weights, mixes, st_out, ro_out, ends, store_sem, end_sem):
    outs = (st_out, ro_out)
    scale = time_step * damping
    copies = []
    for s in range(2):
        first = 0 if s == 0 else 2
        for f in range(FIELDS):
            copies.append(pltpu.make_async_copy(
                partial.at[s, f, pl.ds(first, AX - 2)], outs[s].at[f, pl.ds(first, AX - 2)], store_sem.at[s, f]
            ))
    for copy in copies:
        copy.start()

    for s in range(2):

        def fill(block, carry):
            rows = pl.ds(pl.multiple_of(8 * block, 8), 8)
            mixed = []
            for layer in range(2):
                parts = [ghosts[8 * layer + block, s, g] for g in range(FIELDS)]
                found = []
                for f in range(FIELDS):
                    total = mixes[f * FIELDS] * parts[0]
                    for g in range(1, FIELDS):
                        total = total + mixes[f * FIELDS + g] * parts[g]
                    found.append(total if s == 0 else -total)
                mixed.append(found)
            outer, inner = (15, 14) if s == 0 else (0, 1)
            for f in range(FIELDS):
                total = (4.0 * scale) * mixed[0][f] - scale * mixed[1][f]
                for g in range(FIELDS):
                    term = weights[g * FIELDS + f] * mixed[0][g]
                    total = total + term if s == 0 else total - term
                ends[s, f, outer % 2, rows, :] = partial[s, f, outer, rows, :] + total
                ends[s, f, inner % 2, rows, :] = partial[s, f, inner, rows, :] - scale * mixed[0][f]
            return carry

        lax.fori_loop(0, 8, fill, 0)
        last = pltpu.make_async_copy(ends.at[s], outs[s].at[:, pl.ds(14 if s == 0 else 0, 2)], end_sem.at[s])
        last.start()
        copies.append(last)
    for copy in copies:
        copy.wait()


def close(partial, ghosts, weights, mixes):
    anywhere = pl.BlockSpec(memory_space=pl.ANY)
    whole = pl.BlockSpec(memory_space=pltpu.VMEM)
    dma = pltpu.SemaphoreType.DMA
    shape = jax.ShapeDtypeStruct((FIELDS, AX, ROWS, LANES), f32)
    return pl.pallas_call(
        close_kernel,
        name="close",
        out_shape=(shape, shape),
        in_specs=[whole] * 4,
        out_specs=(anywhere, anywhere),
        scratch_shapes=[pltpu.VMEM((2, FIELDS, 2, ROWS, LANES), f32), dma((2, FIELDS)), dma((2,))],
        compiler_params=pltpu.CompilerParams(vmem_limit_bytes=8 << 20),
    )(partial, ghosts, weights, mixes)


def shards(stator_state, rotor_state, jacobians, field_mix, mode_blend, rotor_offset):
    parts = section(rotor_offset, stator_state, rotor_state, mode_blend, jacobians, field_mix)
    return close(*parts)


def solution(mesh):
    in_specs = (P(None, None, "span", "pitch"), P(None, None, "span", "pitch"), P(), P(), P(), P())
    out_specs = (P(None, None, "span", "pitch"), P(None, None, "span", "pitch"))
    return jax.shard_map(shards, mesh=mesh, in_specs=in_specs, out_specs=out_specs, check_vma=False)
```

time: 60.7 us -> 36.3 us (0.60)
  the two profiles are of different devices: /device:TPU:0 before, /device:TPU:1 now
where the time goes in v2:
time: 36.3 us; the launch traced here: 35.7 us
  Pallas kernels  34.4 us (95%)
  between operations  1.29 us (4%)
    pallas_call x1, Pallas kernels, section(): pl.pallas_call(section_kernel, name='section', out_shape=(pltpu.VMEM((2,...  32 us
    pallas_call x1, Pallas kernels, close(): pl.pallas_call(close_kernel, name='close', out_shape=(shape, shape), in_s...  2.44 us

profile of v2, /device:TPU:1, one launch (start us, length us, event | category | flops | bytes accessed | tf_op | source)
XLA Modules:
  0.0 35.7 jit_solution(10848794989049975260)
XLA Ops:
  1.3 32.0 %section.1 = (f32[2,5,16,64,128]{4,3,2,1,0:T(8,128)S(1)}, f32[16,2,5,8,128]{4,3,2,1,0:T(8,128)S(1)}, f32[75,8,128]{2,1,0:T(8,128)S(1)}, f32[25,8,128]{2,1,0:T(8,128)S(1)}) custom-call(s32[1]{0:T(128)S(6)} %copy.12.off_ref, f32[5,16,64,128]{3,2,1,0:T(8,128)} %st_ref.1, f32[5,16,64,128]{3,2,1,0:T(8,128)} %ro_ref.1, f32[5,2048]{1,0:T(8,128)} %blend_hbm.1, ...), custom_call_target="tpu_custom_call" | custom-call | tf_op jit(solution)/shard_map/section/pallas_call | solution.py:495
  33.3 2.4 %close.1 = (f32[5,16,64,128]{3,2,1,0:T(8,128)}, f32[5,16,64,128]{3,2,1,0:T(8,128)}) custom-call(f32[2,5,16,64,128]{4,3,2,1,0:T(8,128)S(1)} %get-tuple-element.6.partial, f32[16,2,5,8,128]{4,3,2,1,0:T(8,128)S(1)} %get-tuple-element.7.ghosts, f32[75,8,128]{2,1,0:T(8,128)S(1)} %get-tuple-element.8.weights, f32[25,8,128]{2,1,0:T(8,128)S(1)} %get-tuple-element.9.mixes), custom_call_target="tpu_custom_call" | custom-call | tf_op jit(solution)/shard_map/close/pallas_call | solution.py:592

commit v3 on v2

--- a/solution.py
+++ b/solution.py
@@ -16,6 +16,12 @@
 LANES = 128
 TILES = 16
 MESH = pl.DeviceIdType.MESH
+EARLY = 12
+BEFORE = (12,)
+CHUNKS = ((0, 5),)
+ORDER = (
+    (2, 2), (2, 3), (3, 2), (2, 1), (1, 2), (2, 0), (0, 2), (3, 1), (1, 3), (3, 3), (1, 1), (3, 0), (0, 3), (1, 0), (0, 1),
+)
 f32 = jnp.float32
 bf16 = jnp.bfloat16
 
@@ -119,23 +125,24 @@
     off_ref, st_ref, ro_ref, blend_hbm, jac_hbm, mix_hbm, table_hbm, back_hbm, twiddle_hbm, band_hbm,
     partial, ghost_ref, weights, mixes,
     cells, planes, spectrum, blends, turned, outgoing, pitch_pack, pitch_recv, span_pack, span_recv,
-    bent_a, bent_b, edge_fix, permuted, blend_v, jac_v, mix_v, table_ref, back_ref, twiddle_ref, band_ref,
+    bent_a, bent_b, rows_a, rows_b, radial, kept, edge_fix, permuted, blend_v, jac_v, mix_v, table_ref, back_ref, twiddle_ref, band_ref,
     load_sem, own_sem, row_send, row_recv, back_send, back_recv, halo_send, halo_recv, small_sem,
 ):
     me = lax.axis_index("pitch")
     span = lax.axis_index("span")
     left, right = lax.rem(me + 15, 16), lax.rem(me + 1, 16)
+    targets = [4 * lax.rem(me // 4 + dx, 4) + lax.rem(me + dz, 4) for dx, dz in ORDER]
     below, above = lax.rem(span + 7, 8), lax.rem(span + 1, 8)
     states = (st_ref, ro_ref)
 
     def load(s, f):
         return pltpu.make_async_copy(states[s].at[f], cells.at[s, f, pl.ds(2, AX), pl.ds(8, ROWS)], load_sem.at[s, f])
 
-    def row_block(s, target):
+    def row_block(s, target, first=0, count=FIELDS):
         layer, block = target // 8, target % 8
         axial = 15 - layer if s == 0 else layer
         rows = pl.ds(pl.multiple_of(8 * block, 8), 8)
-        return states[s].at[:, axial, rows, :]
+        return states[s].at[pl.ds(first, count), axial, rows, :]
 
     def own_rows(s):
         return pltpu.make_async_copy(row_block(s, me), planes.at[s, me], own_sem.at[s])
@@ -169,28 +176,81 @@
     row = lax.broadcasted_iota(jnp.int32, (8, LANES), 0)
     group = lane % 4
     nothing = jnp.zeros((8, LANES), f32)
+    scale = time_step * damping
     for s in range(2):
         for f in range(FIELDS):
             for t in range(8):
                 for a in (0, 1, 18, 19):
                     cells[s, f, a, 8 + 8 * t:16 + 8 * t, :] = nothing
 
+    for copy in smalls:
+        copy.wait()
+    for d in range(3):
+        for f in range(FIELDS):
+            for g in range(FIELDS):
+                value = jnp.broadcast_to(jac_v[f, d:d + 1, g:g + 1], (8, LANES))
+                weights[(d * FIELDS + g) * FIELDS + f] = (-0.5 * time_step) * value
+    for f in range(FIELDS):
+        for g in range(FIELDS):
+            mixes[f * FIELDS + g] = jnp.broadcast_to(mix_v[f:f + 1, g:g + 1], (8, LANES))
+
+    spot = lax.broadcasted_iota(jnp.int32, (24, 256), 1)
+    field = sum((spot >= 48 * g).astype(jnp.int32) for g in range(1, FIELDS + 1))
+    place = spot - 48 * field
+    for block in range(2):
+        step = place - lax.broadcasted_iota(jnp.int32, (24, 256), 0) - (8 + 8 * block)
+        side = (step == 1).astype(f32) - (step == -1).astype(f32)
+        blur = (4.0 * scale) * (jnp.abs(step) == 1).astype(f32) - scale * (jnp.abs(step) == 2).astype(f32)
+        for f in range(FIELDS):
+            value = jnp.where(field == f, blur, 0.0)
+            for g in range(FIELDS):
+                weight = jnp.broadcast_to(weights[(FIELDS + g) * FIELDS + f][0:1, 0:1], (24, 256))
+                value = value + jnp.where(field == g, weight * side, 0.0)
+            high = value.astype(bf16).astype(f32)
+            low = value - high
+            radial[block, f] = jnp.concatenate([high, low, high], axis=1)
+
+    spare = jnp.zeros((3, LANES), f32)
+    blend_rows = jnp.concatenate(
+        [part for t in range(TILES) for part in (blend_v[:, LANES * t:LANES * t + LANES], spare)], axis=0
+    )
+    source_lane = lax.broadcasted_iota(jnp.int32, (LANES, LANES), 0)
+    target_lane = lax.broadcasted_iota(jnp.int32, (LANES, LANES), 1)
+    chosen = (8 * (source_lane % 16) + source_lane // 16 == target_lane).astype(f32)
+    permuted[...] = jnp.dot(
+        blend_rows, chosen, precision=lax.Precision.HIGHEST, preferred_element_type=f32
+    ).reshape(TILES, 8, LANES)
+
+    def mode_row(k):
+        total = nothing
+        for t in range(TILES):
+            shift = (8 * (t - k)) % LANES
+            value = permuted[t]
+            total = jnp.where(lane // 8 == t, pltpu.roll(value, shift, 1) if shift else value, total)
+        return total
+
+    for c in range(9):
+        near = mode_row(c)
+        other = mode_row(16 - c) if 0 < c < 8 else nothing
+        for f in range(FIELDS):
+            blends[c, f, :, 0:LANES] = jnp.broadcast_to(near[f:f + 1, :], (8, LANES))
+            blends[c, f, :, LANES:] = jnp.broadcast_to(other[f:f + 1, :], (8, LANES))
+
     pl.semaphore_wait(barrier, 17)
 
-    def row_copy(s, target, source):
+    def row_copy(s, chunk, target, source):
+        first, count = CHUNKS[chunk]
         return pltpu.make_async_remote_copy(
-            src_ref=row_block(s, target), dst_ref=planes.at[s, source],
-            send_sem=row_send.at[s, target], recv_sem=row_recv.at[s, source],
+            src_ref=row_block(s, target, first, count), dst_ref=planes.at[s, source, pl.ds(first, count)],
+            send_sem=row_send.at[s, chunk, target], recv_sem=row_recv.at[s, chunk, source],
             device_id={"pitch": target}, device_id_type=MESH,
         )
 
-    def send_rows(j, carry):
-        target = lax.rem(me + j, 16)
-        for s in range(2):
-            row_copy(s, target, me).start()
-        return carry
-
-    lax.fori_loop(1, 16, send_rows, 0)
+    for chunk in range(len(CHUNKS)):
+
+        for target in targets:
+            for s in range(2):
+                row_copy(s, chunk, target, me).start()
 
     def halo_copy(slot, src, dst, where):
         return pltpu.make_async_remote_copy(
@@ -236,43 +296,6 @@
     for copy in (to_above, to_below, to_right, to_left):
         copy.start()
 
-    for copy in smalls:
-        copy.wait()
-    for d in range(3):
-        for f in range(FIELDS):
-            for g in range(FIELDS):
-                value = jnp.broadcast_to(jac_v[f, d:d + 1, g:g + 1], (8, LANES))
-                weights[(d * FIELDS + g) * FIELDS + f] = (-0.5 * time_step) * value
-    for f in range(FIELDS):
-        for g in range(FIELDS):
-            mixes[f * FIELDS + g] = jnp.broadcast_to(mix_v[f:f + 1, g:g + 1], (8, LANES))
-
-    spare = jnp.zeros((3, LANES), f32)
-    blend_rows = jnp.concatenate(
-        [part for t in range(TILES) for part in (blend_v[:, LANES * t:LANES * t + LANES], spare)], axis=0
-    )
-    source_lane = lax.broadcasted_iota(jnp.int32, (LANES, LANES), 0)
-    target_lane = lax.broadcasted_iota(jnp.int32, (LANES, LANES), 1)
-    chosen = (8 * (source_lane % 16) + source_lane // 16 == target_lane).astype(f32)
-    permuted[...] = jnp.dot(
-        blend_rows, chosen, precision=lax.Precision.HIGHEST, preferred_element_type=f32
-    ).reshape(TILES, 8, LANES)
-
-    def mode_row(k):
-        total = nothing
-        for t in range(TILES):
-            shift = (8 * (t - k)) % LANES
-            value = permuted[t]
-            total = jnp.where(lane // 8 == t, pltpu.roll(value, shift, 1) if shift else value, total)
-        return total
-
-    for c in range(9):
-        near = mode_row(c)
-        other = mode_row(16 - c) if 0 < c < 8 else nothing
-        for f in range(FIELDS):
-            blends[c, f, :, 0:LANES] = jnp.broadcast_to(near[f:f + 1, :], (8, LANES))
-            blends[c, f, :, LANES:] = jnp.broadcast_to(other[f:f + 1, :], (8, LANES))
-
     def base_ghosts(block, carry):
         rows = pl.ds(pl.multiple_of(8 + 8 * block, 8), 8)
         for s in range(2):
@@ -287,78 +310,199 @@
 
     lax.fori_loop(0, 8, base_ghosts, 0)
 
+    rim = (lane < 2) | (lane >= LANES - 2)
+
+    def products(layer, bent, rows_out):
+        highs, lows = [], []
+        for k in range(2):
+            s, a = (layer + k) // AX, (layer + k) % AX
+            values = cells[s, :, a + 2, 8:8 + ROWS, :].reshape(FIELDS * ROWS, LANES)
+            high = values.astype(bf16)
+            low = (values - high.astype(f32)).astype(bf16)
+            both = jnp.concatenate([high, low], axis=1)
+            bent[k] = jnp.dot(both, band_ref[...], preferred_element_type=f32).reshape(FIELDS, ROWS, 256)
+            highs.append(high)
+            lows.append(low)
+        blank = jnp.zeros((16, LANES), bf16)
+        for block in range(2):
+
+            def stacked(parts):
+                return jnp.concatenate([
+                    jnp.concatenate(
+                        [part[ROWS * g + 16 * block:ROWS * g + 16 * block + 48, :] for g in range(FIELDS)] + [blank], axis=0
+                    )
+                    for part in parts
+                ], axis=1)
+
+            upper = stacked(highs)
+            data = jnp.concatenate([upper, upper, stacked(lows)], axis=0)
+            left = radial[block].reshape(FIELDS * 24, 768).astype(bf16)
+            rows_out[block] = jnp.dot(left, data, preferred_element_type=f32).reshape(FIELDS, 24, 256)
+
+    def pitch_fix(s, f, a, tile):
+        amount = lax.rem(126 - 32 * lax.rem(a, 4) - 4 * tile + 2 * LANES, LANES)
+        return jnp.where(rim, pltpu.roll(edge_fix[s, f, a // 4], amount, 1), 0.0)
+
+    def sweep(layer, first, rows, bent, fixed):
+        s, a = layer // AX, layer % AX
+        count = rows // 8
+        sums = [None] * FIELDS
+        for g in range(FIELDS):
+
+            def get(axial, radial):
+                start = 8 + first + radial
+                return cells[s, g, a + 2 + axial, start:start + rows, :].reshape(count, 8, LANES)
+
+            ahead, behind = get(1, 0), get(-1, 0)
+            up, down = get(0, 1), get(0, -1)
+            near = (ahead + behind) + (up + down)
+            far = (get(2, 0) + get(-2, 0)) + (get(0, 2) + get(0, -2))
+            own = bent(g)[:, LANES:].reshape(count, 8, LANES) + ((4.0 * scale) * near - scale * far)
+            along = bent(g)[:, 0:LANES].reshape(count, 8, LANES)
+            if fixed:
+                own = own + jnp.stack([pitch_fix(s, g, a, first // 8 + t) for t in range(count)])
+            sums[g] = own if sums[g] is None else sums[g] + own
+            for d, slope in enumerate((ahead - behind, up - down, along)):
+                for f in range(FIELDS):
+                    term = weights[(d * FIELDS + g) * FIELDS + f] * slope
+                    sums[f] = term if sums[f] is None else sums[f] + term
+        for f in range(FIELDS):
+            partial[s, f, a, first:first + rows, :] = sums[f].reshape(rows, LANES)
+
+    def inner(layer, k, bent, rows_in, fixed):
+        s, a = layer // AX, layer % AX
+        sums = [
+            jnp.concatenate([rows_in[block, f, :, LANES * k:LANES * k + LANES] for block in range(2)], axis=0).reshape(6, 8, LANES)
+            for f in range(FIELDS)
+        ]
+        for g in range(FIELDS):
+
+            def get(axial):
+                return cells[s, g, a + 2 + axial, 16:8 + ROWS - 8, :].reshape(6, 8, LANES)
+
+            ahead, behind = get(1), get(-1)
+            along = bent[k, g, 8:ROWS - 8, 0:LANES].reshape(6, 8, LANES)
+            own = bent[k, g, 8:ROWS - 8, LANES:].reshape(6, 8, LANES)
+            own = own + ((4.0 * scale) * (ahead + behind) - scale * (get(2) + get(-2)))
+            if fixed:
+                own = own + jnp.stack([pitch_fix(s, g, a, 1 + t) for t in range(6)])
+            sums[g] = sums[g] + own
+            for d, slope in ((0, ahead - behind), (2, along)):
+                for f in range(FIELDS):
+                    sums[f] = sums[f] + weights[(d * FIELDS + g) * FIELDS + f] * slope
+        for f in range(FIELDS):
+            partial[s, f, a, 8:ROWS - 8, :] = sums[f].reshape(48, LANES)
+
+    def early_layer(layer, k, bent, rows_in):
+        inner(layer, k, bent, rows_in, False)
+        kept[layer, :, 0:8, :] = bent[k, :, 0:8, :]
+        kept[layer, :, 8:16, :] = bent[k, :, ROWS - 8:, :]
+
+    def late_layer(layer, k, bent, rows_in):
+        inner(layer, k, bent, rows_in, True)
+        sweep(layer, 0, 8, lambda g: bent[k, g, 0:8, :], True)
+        sweep(layer, ROWS - 8, 8, lambda g: bent[k, g, ROWS - 8:, :], True)
+
+    def finish_early(layer, carry):
+        s, a = layer // AX, layer % AX
+        sweep(layer, 0, 8, lambda g: kept[layer, g, 0:8, :], True)
+        sweep(layer, ROWS - 8, 8, lambda g: kept[layer, g, 8:16, :], True)
+        for f in range(FIELDS):
+            for t in range(1, 7):
+                partial[s, f, a, 8 * t:8 * t + 8, :] = partial[s, f, a, 8 * t:8 * t + 8, :] + pitch_fix(s, f, a, t)
+        return carry
+
+    def layers(first, last, step):
+        products(first, bent_a, rows_a)
+
+        def four_layers(i, carry):
+            products(4 * i + 2, bent_b, rows_b)
+            step(4 * i, 0, bent_a, rows_a)
+            step(4 * i + 1, 1, bent_a, rows_a)
+            products(jnp.minimum(4 * i + 4, last - 2), bent_a, rows_a)
+            step(4 * i + 2, 0, bent_b, rows_b)
+            step(4 * i + 3, 1, bent_b, rows_b)
+            return carry
+
+        lax.fori_loop(first // 4, last // 4, four_layers, 0)
+
+
     offset = off_ref[0]
     shift, hop = lax.rem(offset, LANES), offset // LANES
 
     for s in range(2):
         own_rows(s).wait()
 
-    def wait_rows(j, carry):
-        source = lax.rem(me + j, 16)
-        for s in range(2):
-            row_copy(s, source, source).wait_recv()
-        return carry
-
-    lax.fori_loop(1, 16, wait_rows, 0)
-
-    def forward(f, carry):
-        for t in range(TILES):
-            turned[t] = pltpu.roll(planes[1, t, f], shift, 1)
-        x = []
-        for t in range(TILES):
-            near = turned[lax.rem(t + 16 - hop, 16)]
-            far = turned[lax.rem(t + 15 - hop, 16)]
-            x.append(jnp.where(lane >= shift, near, far) - planes[0, t, f])
-        cs, ss = forward_16(x)
-        for c in range(9):
-            cosines, sines = twiddle_ref[0, c], twiddle_ref[1, c]
-            if c == 0:
-                real, imaginary = cs[0], nothing
-            elif c == 8:
-                real, imaginary = cs[8] * cosines, -(cs[8] * sines)
-            else:
-                real = cs[c] * cosines - ss[c] * sines
-                imaginary = -(cs[c] * sines + ss[c] * cosines)
-            spectrum[c, f, :, 0:LANES] = real
-            spectrum[c, f, :, LANES:] = imaginary
-        return carry
-
-    lax.fori_loop(0, FIELDS, forward, 0)
-    modes = split_dot(spectrum[...].reshape(9 * 40, 256), table_ref)
-    modes = modes * blends[...].reshape(9 * 40, 256)
-    spectrum[...] = split_dot(modes, back_ref).reshape(9, FIELDS, 8, 256)
-
-    def inverse(f, carry):
-        cs, ss = [], []
-        for c in range(9):
-            cosines, sines = twiddle_ref[0, c], twiddle_ref[1, c]
-            real, imaginary = spectrum[c, f, :, 0:LANES], spectrum[c, f, :, LANES:]
-            cs.append(real * cosines - imaginary * sines)
-            ss.append(-(real * sines + imaginary * cosines))
-        x = inverse_16(cs, ss)
-        for t in range(TILES):
-            outgoing[t, 0, f] = x[t]
-            turned[t] = pltpu.roll(x[t], lax.rem(LANES - shift, LANES), 1)
-        for t in range(TILES):
-            near = turned[lax.rem(t + hop, 16)]
-            far = turned[lax.rem(t + hop + 1, 16)]
-            outgoing[t, 1, f] = jnp.where(lane < LANES - shift, near, far)
-        return carry
-
-    lax.fori_loop(0, FIELDS, inverse, 0)
-
-    def back_copy(target, source):
+    def back_copy(chunk, target, source):
+        first, count = CHUNKS[chunk]
         return pltpu.make_async_remote_copy(
-            src_ref=outgoing.at[target], dst_ref=ghost_ref.at[source],
-            send_sem=back_send.at[target], recv_sem=back_recv.at[source],
+            src_ref=outgoing.at[target, :, pl.ds(first, count)], dst_ref=ghost_ref.at[source, :, pl.ds(first, count)],
+            send_sem=back_send.at[chunk, target], recv_sem=back_recv.at[chunk, source],
             device_id={"pitch": target}, device_id_type=MESH,
         )
 
-    def send_back(j, carry):
-        back_copy(lax.rem(me + j, 16), me).start()
-        return carry
-
-    lax.fori_loop(1, 16, send_back, 0)
+    for chunk, (start, count) in enumerate(CHUNKS):
+        done = sum(BEFORE[:chunk])
+        if BEFORE[chunk]:
+            layers(done, done + BEFORE[chunk], early_layer)
+
+        def wait_rows(j, carry):
+            source = lax.rem(me + j, 16)
+            for s in range(2):
+                row_copy(s, chunk, source, source).wait_recv()
+            return carry
+
+        lax.fori_loop(1, 16, wait_rows, 0)
+
+        def forward(f, carry):
+            for t in range(TILES):
+                turned[t] = pltpu.roll(planes[1, t, f], shift, 1)
+            x = []
+            for t in range(TILES):
+                near = turned[lax.rem(t + 16 - hop, 16)]
+                far = turned[lax.rem(t + 15 - hop, 16)]
+                x.append(jnp.where(lane >= shift, near, far) - planes[0, t, f])
+            cs, ss = forward_16(x)
+            for c in range(9):
+                cosines, sines = twiddle_ref[0, c], twiddle_ref[1, c]
+                if c == 0:
+                    real, imaginary = cs[0], nothing
+                elif c == 8:
+                    real, imaginary = cs[8] * cosines, -(cs[8] * sines)
+                else:
+                    real = cs[c] * cosines - ss[c] * sines
+                    imaginary = -(cs[c] * sines + ss[c] * cosines)
+                spectrum[c, f, :, 0:LANES] = real
+                spectrum[c, f, :, LANES:] = imaginary
+            return carry
+
+        lax.fori_loop(start, start + count, forward, 0)
+        modes = split_dot(spectrum[:, start:start + count].reshape(72 * count, 256), table_ref)
+        modes = modes * blends[:, start:start + count].reshape(72 * count, 256)
+        spectrum[:, start:start + count] = split_dot(modes, back_ref).reshape(9, count, 8, 256)
+
+        def inverse(f, carry):
+            cs, ss = [], []
+            for c in range(9):
+                cosines, sines = twiddle_ref[0, c], twiddle_ref[1, c]
+                real, imaginary = spectrum[c, f, :, 0:LANES], spectrum[c, f, :, LANES:]
+                cs.append(real * cosines - imaginary * sines)
+                ss.append(-(real * sines + imaginary * cosines))
+            x = inverse_16(cs, ss)
+            for t in range(TILES):
+                outgoing[t, 0, f] = x[t]
+                turned[t] = pltpu.roll(x[t], lax.rem(LANES - shift, LANES), 1)
+            for t in range(TILES):
+                near = turned[lax.rem(t + hop, 16)]
+                far = turned[lax.rem(t + hop + 1, 16)]
+                outgoing[t, 1, f] = jnp.where(lane < LANES - shift, near, far)
+            return carry
+
+        lax.fori_loop(start, start + count, inverse, 0)
+
+        for target in targets:
+            back_copy(chunk, target, me).start()
+
     own_back = pltpu.make_async_copy(outgoing.at[me], ghost_ref.at[me], own_sem.at[0])
     own_back.start()
 
@@ -366,7 +510,6 @@
         copy.wait()
     keep_low = jnp.where(span == 0, 0.0, 1.0).astype(f32)
     keep_high = jnp.where(span == 7, 0.0, 1.0).astype(f32)
-    scale = time_step * damping
     for s in range(2):
 
         def unpack(m, carry):
@@ -407,66 +550,18 @@
 
         lax.fori_loop(0, 2, edges, 0)
 
-    rim = (lane < 2) | (lane >= LANES - 2)
-
-    def bend(layer, target):
-        s, a = layer // AX, layer % AX
-        values = cells[s, :, a + 2, 8:8 + ROWS, :].reshape(FIELDS * ROWS, LANES)
-        high = values.astype(bf16)
-        low = (values - high.astype(f32)).astype(bf16)
-        both = jnp.concatenate([high, low], axis=1)
-        target[...] = jnp.dot(both, band_ref[...], preferred_element_type=f32).reshape(FIELDS, ROWS, 256)
-
-    def advance(layer, bent):
-        s, a = layer // AX, layer % AX
-        for half in range(2):
-            start = 8 + 32 * half
-            sums = [None] * FIELDS
-            for g in range(FIELDS):
-
-                def get(axial, radial):
-                    return cells[s, g, a + 2 + axial, start + radial:start + radial + 32, :].reshape(4, 8, LANES)
-
-                ahead, behind = get(1, 0), get(-1, 0)
-                up, down = get(0, 1), get(0, -1)
-                near = (ahead + behind) + (up + down)
-                far = (get(2, 0) + get(-2, 0)) + (get(0, 2) + get(0, -2))
-                along = bent[g, 32 * half:32 * half + 32, 0:LANES].reshape(4, 8, LANES)
-                own = bent[g, 32 * half:32 * half + 32, LANES:].reshape(4, 8, LANES)
-                own = own + ((4.0 * scale) * near - scale * far)
-                fix = edge_fix[s, g, a // 4]
-                base = 126 - 32 * lax.rem(a, 4)
-                own = own + jnp.stack([
-                    jnp.where(rim, pltpu.roll(fix, lax.rem(base - 4 * (4 * half + t) + 2 * LANES, LANES), 1), 0.0)
-                    for t in range(4)
-                ])
-                sums[g] = own if sums[g] is None else sums[g] + own
-                for d, slope in enumerate((ahead - behind, up - down, along)):
-                    for f in range(FIELDS):
-                        term = weights[(d * FIELDS + g) * FIELDS + f] * slope
-                        sums[f] = term if sums[f] is None else sums[f] + term
-            for f in range(FIELDS):
-                partial[s, f, a, 32 * half:32 * half + 32, :] = sums[f].reshape(32, LANES)
-
-    bend(0, bent_a)
-
-    def two_layers(i, carry):
-        bend(2 * i + 1, bent_b)
-        advance(2 * i, bent_a)
-        bend(jnp.minimum(2 * i + 2, 2 * AX - 1), bent_a)
-        advance(2 * i + 1, bent_b)
-        return carry
-
-    lax.fori_loop(0, AX, two_layers, 0)
+    layers(EARLY, 2 * AX, late_layer)
+    lax.fori_loop(0, EARLY, finish_early, 0)
 
     own_back.wait()
 
     def finish(j, carry):
         other = lax.rem(me + j, 16)
-        for s in range(2):
-            row_copy(s, other, me).wait_send()
-        back_copy(other, me).wait_send()
-        back_copy(other, other).wait_recv()
+        for chunk in range(len(CHUNKS)):
+            for s in range(2):
+                row_copy(s, chunk, other, me).wait_send()
+            back_copy(chunk, other, me).wait_send()
+            back_copy(chunk, other, other).wait_recv()
         return carry
 
     lax.fori_loop(1, 16, finish, 0)
@@ -514,8 +609,12 @@
             pltpu.VMEM((2, 2, 10, 8, LANES), f32),
             pltpu.VMEM((2, 2, 20, 8, LANES), f32),
             pltpu.VMEM((2, 2, 20, 8, LANES), f32),
-            pltpu.VMEM((FIELDS, ROWS, 256), f32),
-            pltpu.VMEM((FIELDS, ROWS, 256), f32),
+            pltpu.VMEM((2, FIELDS, ROWS, 256), f32),
+            pltpu.VMEM((2, FIELDS, ROWS, 256), f32),
+            pltpu.VMEM((2, FIELDS, 24, 256), f32),
+            pltpu.VMEM((2, FIELDS, 24, 256), f32),
+            pltpu.VMEM((2, FIELDS, 24, 768), f32),
+            pltpu.VMEM((EARLY, FIELDS, 16, 256), f32),
             pltpu.VMEM((2, FIELDS, 4, 8, LANES), f32),
             pltpu.VMEM((TILES, 8, LANES), f32),
             pltpu.VMEM((FIELDS, NP), f32),
@@ -525,7 +624,8 @@
             pltpu.VMEM((2, 256, 256), bf16),
             pltpu.VMEM((2, 9, 1, LANES), f32),
             pltpu.VMEM((256, 256), bf16),
-            dma((2, FIELDS)), dma((2,)), dma((2, 16)), dma((2, 16)), dma((16,)), dma((16,)), dma((4,)), dma((4,)), dma((7,)),
+            dma((2, FIELDS)), dma((2,)), dma((2, len(CHUNKS), 16)), dma((2, len(CHUNKS), 16)), dma((len(CHUNKS), 16)), dma((len(CHUNKS), 16)),
+            dma((4,)), dma((4,)), dma((7,)),
         ],
         compiler_params=pltpu.CompilerParams(
             collective_id=0, has_side_effects=True, vmem_limit_bytes=32 << 20

time: 36.3 us -> 35.1 us (0.967); the launches traced: 35.7 us -> 35 us
  Pallas kernels: 34.4 us -> 33.7 us
    pallas_call x1, Pallas kernels: 32 us -> 31.2 us  [section(): pl.pallas_call(section_kernel, name='section', out_shape=(pltpu.VMEM((2,...]
where the time goes in v3:
time: 35.1 us; the launch traced here: 35 us
  Pallas kernels  33.7 us (96%)
  between operations  1.29 us (4%)
    pallas_call x1, Pallas kernels, section(): pl.pallas_call(section_kernel, name='section', out_shape=(pltpu.VMEM((2,...  31.2 us
    pallas_call x1, Pallas kernels, close(): pl.pallas_call(close_kernel, name='close', out_shape=(shape, shape), in_s...  2.44 us

profile of v3, /device:TPU:1, one launch (start us, length us, event | category | flops | bytes accessed | tf_op | source)
XLA Modules:
  0.0 35.0 jit_solution(12516424595470476739)
XLA Ops:
  1.3 31.2 %section.1 = (f32[2,5,16,64,128]{4,3,2,1,0:T(8,128)S(1)}, f32[16,2,5,8,128]{4,3,2,1,0:T(8,128)S(1)}, f32[75,8,128]{2,1,0:T(8,128)S(1)}, f32[25,8,128]{2,1,0:T(8,128)S(1)}) custom-call(s32[1]{0:T(128)S(6)} %copy.12.off_ref, f32[5,16,64,128]{3,2,1,0:T(8,128)} %st_ref.1, f32[5,16,64,128]{3,2,1,0:T(8,128)} %ro_ref.1, f32[5,2048]{1,0:T(8,128)} %blend_hbm.1, ...), custom_call_target="tpu_custom_call" | custom-call | tf_op jit(solution)/shard_map/section/pallas_call | solution.py:590
  32.5 2.4 %close.1 = (f32[5,16,64,128]{3,2,1,0:T(8,128)}, f32[5,16,64,128]{3,2,1,0:T(8,128)}) custom-call(f32[2,5,16,64,128]{4,3,2,1,0:T(8,128)S(1)} %get-tuple-element.6.partial, f32[16,2,5,8,128]{4,3,2,1,0:T(8,128)S(1)} %get-tuple-element.7.ghosts, f32[75,8,128]{2,1,0:T(8,128)S(1)} %get-tuple-element.8.weights, f32[25,8,128]{2,1,0:T(8,128)S(1)} %get-tuple-element.9.mixes), custom_call_target="tpu_custom_call" | custom-call | tf_op jit(solution)/shard_map/close/pallas_call | solution.py:692

commit v4 on v3

--- a/solution.py
+++ b/solution.py
@@ -132,6 +132,7 @@
     span = lax.axis_index("span")
     left, right = lax.rem(me + 15, 16), lax.rem(me + 1, 16)
     targets = [4 * lax.rem(me // 4 + dx, 4) + lax.rem(me + dz, 4) for dx, dz in ORDER]
+    sources = [4 * lax.rem(me // 4 + 4 - dx, 4) + lax.rem(me + 4 - dz, 4) for dx, dz in ORDER]
     below, above = lax.rem(span + 7, 8), lax.rem(span + 1, 8)
     states = (st_ref, ro_ref)
 
@@ -446,21 +447,21 @@
         if BEFORE[chunk]:
             layers(done, done + BEFORE[chunk], early_layer)
 
-        def wait_rows(j, carry):
-            source = lax.rem(me + j, 16)
+        def turn(source):
+            for f in range(start, start + count):
+                turned[source, f] = pltpu.roll(planes[1, source, f], shift, 1)
+
+        turn(me)
+        for source in sources:
             for s in range(2):
                 row_copy(s, chunk, source, source).wait_recv()
-            return carry
-
-        lax.fori_loop(1, 16, wait_rows, 0)
+            turn(source)
 
         def forward(f, carry):
-            for t in range(TILES):
-                turned[t] = pltpu.roll(planes[1, t, f], shift, 1)
             x = []
             for t in range(TILES):
-                near = turned[lax.rem(t + 16 - hop, 16)]
-                far = turned[lax.rem(t + 15 - hop, 16)]
+                near = turned[lax.rem(t + 16 - hop, 16), f]
+                far = turned[lax.rem(t + 15 - hop, 16), f]
                 x.append(jnp.where(lane >= shift, near, far) - planes[0, t, f])
             cs, ss = forward_16(x)
             for c in range(9):
@@ -476,7 +477,7 @@
                 spectrum[c, f, :, LANES:] = imaginary
             return carry
 
-        lax.fori_loop(start, start + count, forward, 0)
+        lax.fori_loop(start, start + count, forward, 0, unroll=True)
         modes = split_dot(spectrum[:, start:start + count].reshape(72 * count, 256), table_ref)
         modes = modes * blends[:, start:start + count].reshape(72 * count, 256)
         spectrum[:, start:start + count] = split_dot(modes, back_ref).reshape(9, count, 8, 256)
@@ -491,14 +492,14 @@
             x = inverse_16(cs, ss)
             for t in range(TILES):
                 outgoing[t, 0, f] = x[t]
-                turned[t] = pltpu.roll(x[t], lax.rem(LANES - shift, LANES), 1)
+                turned[t, f] = pltpu.roll(x[t], lax.rem(LANES - shift, LANES), 1)
             for t in range(TILES):
-                near = turned[lax.rem(t + hop, 16)]
-                far = turned[lax.rem(t + hop + 1, 16)]
+                near = turned[lax.rem(t + hop, 16), f]
+                far = turned[lax.rem(t + hop + 1, 16), f]
                 outgoing[t, 1, f] = jnp.where(lane < LANES - shift, near, far)
             return carry
 
-        lax.fori_loop(start, start + count, inverse, 0)
+        lax.fori_loop(start, start + count, inverse, 0, unroll=True)
 
         for target in targets:
             back_copy(chunk, target, me).start()
@@ -603,7 +604,7 @@
             pltpu.VMEM((2, 16, FIELDS, 8, LANES), f32),
             pltpu.VMEM((9, FIELDS, 8, 256), f32),
             pltpu.VMEM((9, FIELDS, 8, 256), f32),
-            pltpu.VMEM((16, 8, LANES), f32),
+            pltpu.VMEM((16, FIELDS, 8, LANES), f32),
             pltpu.VMEM((16, 2, FIELDS, 8, LANES), f32),
             pltpu.VMEM((2, 2, 10, 8, LANES), f32),
             pltpu.VMEM((2, 2, 10, 8, LANES), f32),

time: 35.1 us -> 35.1 us (level)
  no operation moved by 1% of the time
where the time goes in v4:
time: 35.1 us; the launch traced here: 35 us
  Pallas kernels  33.7 us (96%)
  between operations  1.29 us (4%)
    pallas_call x1, Pallas kernels, section(): pl.pallas_call(section_kernel, name='section', out_shape=(pltpu.VMEM((2,...  31.3 us
    pallas_call x1, Pallas kernels, close(): pl.pallas_call(close_kernel, name='close', out_shape=(shape, shape), in_s...  2.44 us

profile of v4, /device:TPU:1, one launch (start us, length us, event | category | flops | bytes accessed | tf_op | source)
XLA Modules:
  0.0 35.0 jit_solution(11764389706674370072)
XLA Ops:
  1.3 31.3 %section.1 = (f32[2,5,16,64,128]{4,3,2,1,0:T(8,128)S(1)}, f32[16,2,5,8,128]{4,3,2,1,0:T(8,128)S(1)}, f32[75,8,128]{2,1,0:T(8,128)S(1)}, f32[25,8,128]{2,1,0:T(8,128)S(1)}) custom-call(s32[1]{0:T(128)S(6)} %copy.12.off_ref, f32[5,16,64,128]{3,2,1,0:T(8,128)} %st_ref.1, f32[5,16,64,128]{3,2,1,0:T(8,128)} %ro_ref.1, f32[5,2048]{1,0:T(8,128)} %blend_hbm.1, ...), custom_call_target="tpu_custom_call" | custom-call | tf_op jit(solution)/shard_map/section/pallas_call | solution.py:591
  32.6 2.4 %close.1 = (f32[5,16,64,128]{3,2,1,0:T(8,128)}, f32[5,16,64,128]{3,2,1,0:T(8,128)}) custom-call(f32[2,5,16,64,128]{4,3,2,1,0:T(8,128)S(1)} %get-tuple-element.6.partial, f32[16,2,5,8,128]{4,3,2,1,0:T(8,128)S(1)} %get-tuple-element.7.ghosts, f32[75,8,128]{2,1,0:T(8,128)S(1)} %get-tuple-element.8.weights, f32[25,8,128]{2,1,0:T(8,128)S(1)} %get-tuple-element.9.mixes), custom_call_target="tpu_custom_call" | custom-call | tf_op jit(solution)/shard_map/close/pallas_call | solution.py:693

commit v5 on v4

--- a/solution.py
+++ b/solution.py
@@ -344,31 +344,33 @@
         amount = lax.rem(126 - 32 * lax.rem(a, 4) - 4 * tile + 2 * LANES, LANES)
         return jnp.where(rim, pltpu.roll(edge_fix[s, f, a // 4], amount, 1), 0.0)
 
-    def sweep(layer, first, rows, bent, fixed):
+    def rim_tiles(layer, bent):
         s, a = layer // AX, layer % AX
-        count = rows // 8
         sums = [None] * FIELDS
         for g in range(FIELDS):
 
             def get(axial, radial):
-                start = 8 + first + radial
-                return cells[s, g, a + 2 + axial, start:start + rows, :].reshape(count, 8, LANES)
+                low, high = 8 + radial, ROWS + radial
+                return jnp.stack([
+                    cells[s, g, a + 2 + axial, low:low + 8, :], cells[s, g, a + 2 + axial, high:high + 8, :],
+                ])
 
             ahead, behind = get(1, 0), get(-1, 0)
             up, down = get(0, 1), get(0, -1)
             near = (ahead + behind) + (up + down)
             far = (get(2, 0) + get(-2, 0)) + (get(0, 2) + get(0, -2))
-            own = bent(g)[:, LANES:].reshape(count, 8, LANES) + ((4.0 * scale) * near - scale * far)
-            along = bent(g)[:, 0:LANES].reshape(count, 8, LANES)
-            if fixed:
-                own = own + jnp.stack([pitch_fix(s, g, a, first // 8 + t) for t in range(count)])
+            pitch = bent(g)
+            along = pitch[:, 0:LANES].reshape(2, 8, LANES)
+            own = pitch[:, LANES:].reshape(2, 8, LANES) + ((4.0 * scale) * near - scale * far)
+            own = own + jnp.stack([pitch_fix(s, g, a, 0), pitch_fix(s, g, a, 7)])
             sums[g] = own if sums[g] is None else sums[g] + own
             for d, slope in enumerate((ahead - behind, up - down, along)):
                 for f in range(FIELDS):
                     term = weights[(d * FIELDS + g) * FIELDS + f] * slope
                     sums[f] = term if sums[f] is None else sums[f] + term
         for f in range(FIELDS):
-            partial[s, f, a, first:first + rows, :] = sums[f].reshape(rows, LANES)
+            partial[s, f, a, 0:8, :] = sums[f][0]
+            partial[s, f, a, ROWS - 8:ROWS, :] = sums[f][1]
 
     def inner(layer, k, bent, rows_in, fixed):
         s, a = layer // AX, layer % AX
@@ -401,13 +403,11 @@
 
     def late_layer(layer, k, bent, rows_in):
         inner(layer, k, bent, rows_in, True)
-        sweep(layer, 0, 8, lambda g: bent[k, g, 0:8, :], True)
-        sweep(layer, ROWS - 8, 8, lambda g: bent[k, g, ROWS - 8:, :], True)
+        rim_tiles(layer, lambda g: jnp.concatenate([bent[k, g, 0:8, :], bent[k, g, ROWS - 8:, :]], axis=0))
 
     def finish_early(layer, carry):
         s, a = layer // AX, layer % AX
-        sweep(layer, 0, 8, lambda g: kept[layer, g, 0:8, :], True)
-        sweep(layer, ROWS - 8, 8, lambda g: kept[layer, g, 8:16, :], True)
+        rim_tiles(layer, lambda g: kept[layer, g])
         for f in range(FIELDS):
             for t in range(1, 7):
                 partial[s, f, a, 8 * t:8 * t + 8, :] = partial[s, f, a, 8 * t:8 * t + 8, :] + pitch_fix(s, f, a, t)

time: 35.1 us -> 35.1 us (level)
  no operation moved by 1% of the time
where the time goes in v5:
time: 35.1 us; the launch traced here: 35 us
  Pallas kernels  33.7 us (96%)
  between operations  1.29 us (4%)
    pallas_call x1, Pallas kernels, section(): pl.pallas_call(section_kernel, name='section', out_shape=(pltpu.VMEM((2,...  31.3 us
    pallas_call x1, Pallas kernels, close(): pl.pallas_call(close_kernel, name='close', out_shape=(shape, shape), in_s...  2.44 us

profile of v5, /device:TPU:1, one launch (start us, length us, event | category | flops | bytes accessed | tf_op | source)
XLA Modules:
  0.0 35.0 jit_solution(11046603185689267711)
XLA Ops:
  1.3 31.3 %section.1 = (f32[2,5,16,64,128]{4,3,2,1,0:T(8,128)S(1)}, f32[16,2,5,8,128]{4,3,2,1,0:T(8,128)S(1)}, f32[75,8,128]{2,1,0:T(8,128)S(1)}, f32[25,8,128]{2,1,0:T(8,128)S(1)}) custom-call(s32[1]{0:T(128)S(6)} %copy.12.off_ref, f32[5,16,64,128]{3,2,1,0:T(8,128)} %st_ref.1, f32[5,16,64,128]{3,2,1,0:T(8,128)} %ro_ref.1, f32[5,2048]{1,0:T(8,128)} %blend_hbm.1, ...), custom_call_target="tpu_custom_call" | custom-call | tf_op jit(solution)/shard_map/section/pallas_call | solution.py:591
  32.5 2.4 %close.1 = (f32[5,16,64,128]{3,2,1,0:T(8,128)}, f32[5,16,64,128]{3,2,1,0:T(8,128)}) custom-call(f32[2,5,16,64,128]{4,3,2,1,0:T(8,128)S(1)} %get-tuple-element.6.partial, f32[16,2,5,8,128]{4,3,2,1,0:T(8,128)S(1)} %get-tuple-element.7.ghosts, f32[75,8,128]{2,1,0:T(8,128)S(1)} %get-tuple-element.8.weights, f32[25,8,128]{2,1,0:T(8,128)S(1)} %get-tuple-element.9.mixes), custom_call_target="tpu_custom_call" | custom-call | tf_op jit(solution)/shard_map/close/pallas_call | solution.py:693

commit v6 on v5

--- a/solution.py
+++ b/solution.py
@@ -16,8 +16,8 @@
 LANES = 128
 TILES = 16
 MESH = pl.DeviceIdType.MESH
-EARLY = 12
-BEFORE = (12,)
+EARLY = 16
+BEFORE = (16,)
 CHUNKS = ((0, 5),)
 ORDER = (
     (2, 2), (2, 3), (3, 2), (2, 1), (1, 2), (2, 0), (0, 2), (3, 1), (1, 3), (3, 3), (1, 1), (3, 0), (0, 3), (1, 0), (0, 1),

time: 35.1 us -> 34.3 us (0.977)
  Pallas kernels: 33.7 us -> 32.9 us
    pallas_call x1, Pallas kernels: 31.3 us -> 30.5 us  [section(): pl.pallas_call(section_kernel, name='section', out_shape=(pltpu.VMEM((2,...]
where the time goes in v6:
time: 34.3 us; the launch traced here: 34.2 us
  Pallas kernels  32.9 us (96%)
  between operations  1.29 us (4%)
    pallas_call x1, Pallas kernels, section(): pl.pallas_call(section_kernel, name='section', out_shape=(pltpu.VMEM((2,...  30.5 us
    pallas_call x1, Pallas kernels, close(): pl.pallas_call(close_kernel, name='close', out_shape=(shape, shape), in_s...  2.44 us

profile of v6, /device:TPU:1, one launch (start us, length us, event | category | flops | bytes accessed | tf_op | source)
XLA Modules:
  0.0 34.2 jit_solution(2153928613809524028)
XLA Ops:
  1.3 30.5 %section.1 = (f32[2,5,16,64,128]{4,3,2,1,0:T(8,128)S(1)}, f32[16,2,5,8,128]{4,3,2,1,0:T(8,128)S(1)}, f32[75,8,128]{2,1,0:T(8,128)S(1)}, f32[25,8,128]{2,1,0:T(8,128)S(1)}) custom-call(s32[1]{0:T(128)S(6)} %copy.12.off_ref, f32[5,16,64,128]{3,2,1,0:T(8,128)} %st_ref.1, f32[5,16,64,128]{3,2,1,0:T(8,128)} %ro_ref.1, f32[5,2048]{1,0:T(8,128)} %blend_hbm.1, ...), custom_call_target="tpu_custom_call" | custom-call | tf_op jit(solution)/shard_map/section/pallas_call | solution.py:591
  31.7 2.4 %close.1 = (f32[5,16,64,128]{3,2,1,0:T(8,128)}, f32[5,16,64,128]{3,2,1,0:T(8,128)}) custom-call(f32[2,5,16,64,128]{4,3,2,1,0:T(8,128)S(1)} %get-tuple-element.6.partial, f32[16,2,5,8,128]{4,3,2,1,0:T(8,128)S(1)} %get-tuple-element.7.ghosts, f32[75,8,128]{2,1,0:T(8,128)S(1)} %get-tuple-element.8.weights, f32[25,8,128]{2,1,0:T(8,128)S(1)} %get-tuple-element.9.mixes), custom_call_target="tpu_custom_call" | custom-call | tf_op jit(solution)/shard_map/close/pallas_call | solution.py:693
